TPU v7x, 32 devices: a whole 2x2x4 slice. The times are simulated.
32 devices in a mesh: ctx: 8 (over z, y), head: 4 (over x, core).
Axes of the slice: x: 2, y: 2, z: 4, core: 2. Of those that a mesh axis runs over, the one named last changes fastest.
Arguments:
- queries: bfloat16 [2048, 12288], P(('ctx', 'head')), may hold values from -96 to 96
- key_rows: bfloat16 [2048, 768], P(('ctx', 'head')), may hold values from -8 to 8
- values: bfloat16 [2048, 512], P(('ctx', 'head')), may hold values from -6 to 6
- gate_logits: bfloat16 [2048, 128], P(('ctx', 'head')), may hold values from -6 to 6
- key_mix: bfloat16 [4, 32, 192], replicated, may hold values from -1 to 1
- key_proj: bfloat16 [4, 192, 192], replicated, may hold values from -1 to 1
- value_mix: bfloat16 [4, 32, 128], replicated, may hold values from -1 to 1
- value_proj: bfloat16 [4, 128, 128], replicated, may hold values from -0.5 to 0.5
Outputs:
- mixture: bfloat16 [2048, 8192], P(('ctx', 'head'))
All inputs are finite; a program needn't handle non-finite values.
Results may differ from a plain program's by a relative error of at most 0.012.
Values may be sent and summed in bfloat16 or wider, within the bound.
No kernel may reach another device: no remote copies, remote signals or barrier semaphores. Data moves between devices by JAX's collectives and lax.ppermute only.
A program may use at most 64 MiB of HBM per device.

v0:
```python
import math

import jax
import jax.numpy as jnp
from jax import lax
from jax.sharding import PartitionSpec as P

QHEADS = 64
GROUPS = 4
KDIM = 192
VDIM = 128
BLOCK = 32
STRIDE = 16
WINDOW = 512


def passed_along(value, axis, steps):
    count = lax.axis_size(axis)
    leading, last = (max(0, -steps), min(count, count - steps))
    return lax.ppermute(value, axis, [(source, source + steps) for source in range(leading, last)])


def compress_block(rows, mixer, projection):
    block_count = rows.shape[0] // STRIDE - 1
    halves = rows.reshape(block_count + 1, STRIDE, rows.shape[1], rows.shape[2])
    pooled = jnp.einsum(
        "bjgd,gjd->bgd", halves[:-1], mixer[:, :STRIDE], preferred_element_type=jnp.float32
    )
    pooled = pooled + jnp.einsum(
        "bjgd,gjd->bgd", halves[1:], mixer[:, STRIDE:], preferred_element_type=jnp.float32
    )
    summary = jnp.einsum(
        "bgd,gde->bge", pooled.astype(jnp.bfloat16), projection, preferred_element_type=jnp.float32
    )
    return summary.astype(jnp.bfloat16)


def soft_mix(scores, visible, value_rows):
    masked = jnp.where(visible, scores, -1e30)
    highest = jnp.max(masked, axis=-1, keepdims=True)
    weights = jnp.where(visible, jnp.exp(scores - highest), 0.0)
    weight_total = jnp.sum(weights, axis=-1)
    numerator = jnp.einsum(
        "tghs,sgd->tghd",
        weights.astype(jnp.bfloat16),
        value_rows,
        preferred_element_type=jnp.float32,
    )
    safe_total = jnp.where(weight_total > 0.0, weight_total, 1.0)
    return numerator / safe_total[..., None]


def attend(
    query_rows,
    own_keys,
    own_values,
    gate_rows,
    key_mix,
    key_proj,
    value_mix,
    value_proj,
    group_count,
    query_offset,
):
    per_group = QHEADS // GROUPS
    row_count = query_rows.shape[0]
    block_rows = own_keys.shape[0]
    score_scale = 1.0 / math.sqrt(KDIM)
    queried = query_rows.reshape(row_count, group_count, per_group, KDIM)
    block_keys = own_keys.reshape(block_rows, group_count, KDIM)
    block_values = own_values.reshape(block_rows, group_count, VDIM)
    block_first = lax.axis_index("ctx") * block_rows
    positions = block_first + query_offset + jnp.arange(row_count, dtype=jnp.int32)
    next_keys, next_values = passed_along((block_keys[:STRIDE], block_values[:STRIDE]), "ctx", -1)
    summary_keys = compress_block(jnp.concatenate([block_keys, next_keys], 0), key_mix, key_proj)
    summary_values = compress_block(
        jnp.concatenate([block_values, next_values], 0), value_mix, value_proj
    )
    distance_count = -(-WINDOW // block_rows)
    near_keys = []
    near_values = []
    for distance in range(distance_count, 0, -1):
        far_keys, far_values = passed_along((block_keys, block_values), "ctx", distance)
        near_keys.append(far_keys)
        near_values.append(far_values)
    near_keys.append(block_keys)
    near_values.append(block_values)
    near_keys = jnp.concatenate(near_keys, 0)
    near_values = jnp.concatenate(near_values, 0)
    key_places = (
        block_first - distance_count * block_rows + jnp.arange(near_keys.shape[0], dtype=jnp.int32)
    )
    near_visible = (
        (key_places[None, :] <= positions[:, None])
        & (key_places[None, :] > positions[:, None] - WINDOW)
        & (key_places[None, :] >= 0)
    )
    scores = (
        jnp.einsum("tghd,sgd->tghs", queried, near_keys, preferred_element_type=jnp.float32)
        * score_scale
    )
    window_out = soft_mix(scores, near_visible[:, None, None, :], near_values)

    def absorb_part(running, portion, offset):
        part_keys, part_values = portion
        block_ends = (offset + jnp.arange(part_keys.shape[0], dtype=jnp.int32)) * STRIDE + BLOCK - 1
        visible = (block_ends[None, :] <= positions[:, None])[:, None, None, :]
        highest, weight_total, numerator = running
        part_scores = (
            jnp.einsum("tghd,bgd->tghb", queried, part_keys, preferred_element_type=jnp.float32)
            * score_scale
        )
        masked = jnp.where(visible, part_scores, -1e30)
        new_highest = jnp.maximum(highest, jnp.max(masked, axis=-1))
        weights = jnp.where(visible, jnp.exp(part_scores - new_highest[..., None]), 0.0)
        factor = jnp.exp(highest - new_highest)
        weight_total = weight_total * factor + jnp.sum(weights, axis=-1)
        numerator = numerator * factor[..., None] + jnp.einsum(
            "tghb,bgd->tghd",
            weights.astype(jnp.bfloat16),
            part_values,
            preferred_element_type=jnp.float32,
        )
        return (new_highest, weight_total, numerator)

    def absorb(running, portion, offset):
        part_count = portion[0].shape[0]
        if part_count > 256 and part_count % 256 == 0:

            def step(step_index, state):
                sub_keys = lax.dynamic_slice_in_dim(portion[0], step_index * 256, 256, 0)
                sub_values = lax.dynamic_slice_in_dim(portion[1], step_index * 256, 256, 0)
                return absorb_part(state, (sub_keys, sub_values), offset + step_index * 256)

            return lax.fori_loop(0, part_count // 256, step, running)
        return absorb_part(running, portion, offset)

    initial = (
        jnp.full((row_count, group_count, per_group), -1e30, jnp.float32),
        jnp.zeros((row_count, group_count, per_group), jnp.float32),
        jnp.zeros((row_count, group_count, per_group, VDIM), jnp.float32),
    )
    highest, weight_total, numerator = absorb(
        initial,
        (
            lax.all_gather(summary_keys, "ctx", axis=0, tiled=True),
            lax.all_gather(summary_values, "ctx", axis=0, tiled=True),
        ),
        jnp.int32(0),
    )
    compressed_out = numerator / jnp.where(weight_total > 0.0, weight_total, 1.0)[..., None]
    gate_values = jax.nn.sigmoid(
        gate_rows.reshape(row_count, group_count, per_group, 2).astype(jnp.float32)
    )
    mixture = gate_values[..., 0:1] * compressed_out + gate_values[..., 1:2] * window_out
    return mixture.astype(jnp.bfloat16).reshape(row_count, group_count * per_group * VDIM)


def local(queries, key_rows, values, gate_logits, key_mix, key_proj, value_mix, value_proj):
    own_keys, own_values = (
        lax.all_gather(key_rows, "head", axis=0, tiled=True),
        lax.all_gather(values, "head", axis=0, tiled=True),
    )
    group_count = GROUPS
    query_offset = lax.axis_index("head") * queries.shape[0]
    mixture = attend(
        queries,
        own_keys,
        own_values,
        gate_logits,
        key_mix,
        key_proj,
        value_mix,
        value_proj,
        group_count,
        query_offset,
    )
    return mixture


def solution(mesh):
    placed = (
        P(("ctx", "head"), None),
        P(("ctx", "head"), None),
        P(("ctx", "head"), None),
        P(("ctx", "head"), None),
        P(),
        P(),
        P(),
        P(),
    )
    return jax.shard_map(
        local, mesh=mesh, in_specs=placed, out_specs=P(("ctx", "head"), None), check_vma=False
    )
```

profile of v0, /device:TPU:0, one launch (start us, length us, event | category | flops | bytes accessed | tf_op | source)
XLA Modules:
  0.0 140.7 jit_solution(7541661205910600082)
XLA Ops:
  0.0 0.0 copy-start
  0.0 0.0 copy-start.4
  0.0 8.3 %all_gather.12 = bf16[256,768]{1,0:T(8,128)(2,1)S(1)} all-gather(bf16[64,768]{1,0:T(8,128)(2,1)} %param.9), channel_id=1, replica_groups=mesh['ctx'=8,'head'=4] {'head'}, dimensions={0}, use_global_device_ids=true | all-gather | bytes 491520 | tf_op jit(solution)/shard_map/all_gather | solution.py:161
  8.3 0.0 copy-start.6
  8.3 0.2 copy.57
  8.4 4.2 %collective-permute-start.4 = (bf16[256,4,192]{0,2,1:T(8,128)(2,1)S(1)}, bf16[256,4,192]{0,2,1:T(8,128)(2,1)}, u32[]{:S(2)}, u32[]{:S(2)}) collective-permute-start(bf16[256,4,192]{0,2,1:T(8,128)(2,1)S(1)} %bitcast.114), channel_id=1, source_target_pairs={{0,8},{4,12},{8,16},{12,20},{16,24},{20,28},{1,9},{5,13},{9,17},{1... | collective-permute-start | bytes 1179656 | tf_op jit(solution)/shard_map/ppermute | solution.py:20
  12.7 4.2 %collective-permute-start.5 = (bf16[256,4,192]{0,2,1:T(8,128)(2,1)S(1)}, bf16[256,4,192]{0,2,1:T(8,128)(2,1)}, u32[]{:S(2)}, u32[]{:S(2)}) collective-permute-start(bf16[256,4,192]{0,2,1:T(8,128)(2,1)S(1)} %bitcast.115), channel_id=1, source_target_pairs={{0,4},{4,8},{8,12},{12,16},{16,20},{20,24},{24,28},{1,5},{5,9},{9,... | collective-permute-start | bytes 1179656 | tf_op jit(solution)/shard_map/ppermute | solution.py:20
  16.8 6.0 %all_gather.14 = bf16[256,512]{1,0:T(8,128)(2,1)S(1)} all-gather(bf16[64,512]{1,0:T(8,128)(2,1)} %param.10), channel_id=1, replica_groups=mesh['ctx'=8,'head'=4] {'head'}, dimensions={0}, use_global_device_ids=true | all-gather | bytes 327680 | tf_op jit(solution)/shard_map/all_gather | solution.py:162
  22.8 0.1 copy.61
  23.0 0.8 copy.64
  23.8 2.8 %collective-permute-start.2 = (bf16[256,4,128]{2,0,1:T(8,128)(2,1)}, bf16[256,4,128]{2,0,1:T(8,128)(2,1)}, u32[]{:S(2)}, u32[]{:S(2)}) collective-permute-start(bf16[256,4,128]{2,0,1:T(8,128)(2,1)} %copy.64), channel_id=1, source_target_pairs={{0,8},{4,12},{8,16},{12,20},{16,24},{20,28},{1,9},{5,13},{9,17},{1... | collective-permute-start | bytes 786440 | tf_op jit(solution)/shard_map/ppermute | solution.py:20
  26.6 4.1 %collective-permute-start.3 = (bf16[256,4,128]{2,0,1:T(8,128)(2,1)}, bf16[256,4,128]{2,0,1:T(8,128)(2,1)}, u32[]{:S(2)}, u32[]{:S(2)}) collective-permute-start(bf16[256,4,128]{2,0,1:T(8,128)(2,1)} %copy.64), channel_id=1, source_target_pairs={{0,4},{4,8},{8,12},{12,16},{16,20},{20,24},{24,28},{1,5},{5,9},{9,... | collective-permute-start | bytes 786440 | tf_op jit(solution)/shard_map/ppermute | solution.py:20
  30.7 0.8 copy.104
  31.4 1.3 collective-permute-start.1
  32.7 0.5 slice.51
  33.2 0.1 slice.58
  33.3 0.0 copy-done.4
  33.4 0.6 bitcast_convert_fusion.1
  34.0 0.0 copy-done.6
  34.0 0.6 bitcast_convert_fusion.3
  34.7 0.0 copy-done.9
  34.7 0.1 copy.56
  34.8 0.7 fusion.56
  35.5 0.9 multiply_reduce_fusion.1
  36.4 0.1 broadcast_compare_fusion
  36.5 0.7 and_and_fusion
  37.2 0.8 multiply_reduce_fusion.3
  38.0 0.8 copy.58
  38.8 3.6 %reshape.152 = bf16[64,4,16,192]{3,2,1,0:T(8,128)(2,1)S(1)} reshape(bf16[64,12288]{1,0:T(8,128)(2,1)} %param.8) | data formatting | bytes 3145728 | tf_op jit(solution)/shard_map/reshape | solution.py:69
  42.4 0.0 collective-permute-done.1
  42.4 1.3 collective-permute-start
  43.7 1.8 %pad_maximum_fusion.1 = bf16[256,4,128]{0,2,1:T(8,128)(2,1)} fusion(bf16[16,4,128]{0,2,1:T(8,128)(2,1)} %collective-permute-done.1, bf16[256,4,128]{0,2,1:T(8,128)(2,1)S(1)} %bitcast.119), kind=kLoop, calls=%fused_computation.55 | loop fusion | flops 524288 | bytes 540672 | tf_op jit(solution)/shard_map/concatenate | solution.py:77
  45.5 1.1 copy.105
  46.6 0.0 copy-done.2
  46.6 0.1 multiply_reduce_fusion.2
  46.7 0.0 copy-done.3
  46.7 1.0 fusion.31
  47.8 32.0 %all_gather.15 = bf16[128,4,128]{2,0,1:T(8,128)(2,1)S(1)} all-gather(bf16[16,4,128]{2,0,1:T(8,128)(2,1)S(1)} %fusion.31), channel_id=1, replica_groups=mesh['ctx'=8,'head'=4] {'ctx'}, dimensions={0}, use_global_device_ids=true | all-gather | bytes 147456 | tf_op jit(solution)/shard_map/all_gather | solution.py:147
  79.8 0.0 collective-permute-done
  79.8 1.9 %pad_maximum_fusion = bf16[256,4,192]{0,2,1:T(8,128)(2,1)} fusion(bf16[16,4,192]{0,2,1:T(8,128)(2,1)} %collective-permute-done, bf16[256,4,192]{0,2,1:T(8,128)(2,1)S(1)} %bitcast.116), kind=kLoop, calls=%fused_computation.54 | loop fusion | flops 786432 | bytes 811008 | tf_op jit(solution)/shard_map/concatenate | solution.py:75
  81.7 1.2 copy.103
  82.9 1.1 multiply_reduce_fusion
  84.0 0.0 copy-done
  84.0 1.0 fusion.30
  85.0 30.7 %all_gather.13 = bf16[128,4,192]{2,0,1:T(8,128)(2,1)S(1)} all-gather(bf16[16,4,192]{2,0,1:T(8,128)(2,1)S(1)} %fusion.30), channel_id=1, replica_groups=mesh['ctx'=8,'head'=4] {'ctx'}, dimensions={0}, use_global_device_ids=true | all-gather | bytes 221184 | tf_op jit(solution)/shard_map/all_gather | solution.py:146
  115.7 2.7 %fusion.15 = (f32[64,4,16]{0,2,1:T(8,128)S(1)}, f32[4,128,64,16]{1,2,3,0:T(8,128)S(1)}) fusion(pred[64,128]{1,0:T(8,128)(4,1)S(1)} %broadcast_compare_fusion, bf16[64,4,16,192]{3,2,1,0:T(8,128)(2,1)S(1)} %reshape.152, bf16[128,4,192]{2,0,1:T(8,128)(2,1)S(1)} %all_gather.13), kind=kOutput, calls=%fused_computation.21 | convolution fusion | flops 202895360 | bytes 3891200 | tf_op jit(solution)/shard_map/tghd,bgd->tghb/dot_general | solution.py:110
  118.4 1.5 %fusion.24 = f32[64,4,16]{0,2,1:T(8,128)S(1)} fusion(f32[4,128,64,16]{1,2,3,0:T(8,128)S(1)} %get-tuple-element.14, f32[64,4,16]{0,2,1:T(8,128)S(1)} %broadcast_maximum_fusion, pred[64,128]{1,0:T(8,128)(4,1)S(1)} %broadcast_compare_fusion), kind=kLoop, calls=%fused_computation.28 | loop fusion | flops 2093056 | bytes 2138112 | tf_op jit(solution)/shard_map/reduce_sum | solution.py:117
  120.0 2.0 %fusion.32 = f32[4,128,64,16]{1,2,3,0:T(8,128)} fusion(f32[4,128,64,16]{1,2,3,0:T(8,128)S(1)} %get-tuple-element.14, f32[64,4,16]{0,2,1:T(8,128)S(1)} %broadcast_maximum_fusion, pred[64,128]{1,0:T(8,128)(4,1)S(1)} %broadcast_compare_fusion, bf16[128,4,128]{2,0,1:T(8,128)(2,1)S(1)} %all_gather.15), kind=kOutput, calls=%fused_computation.39 | convolution fusion | flops 136314880 | bytes 4349952 | tf_op jit(solution)/shard_map/tghb,bgd->tghd/dot_general | solution.py:118
  122.0 0.0 collective-permute-done.4
  122.0 0.0 collective-permute-done.5
  122.0 3.4 %fusion.18 = f32[4,768,64,16]{1,2,3,0:T(8,128)S(1)} fusion(bf16[64,4,16,192]{3,2,1,0:T(8,128)(2,1)S(1)} %reshape.152, bf16[256,4,192]{0,2,1:T(8,128)(2,1)S(1)} %bitcast.117, bf16[256,4,192]{0,2,1:T(8,128)(2,1)} %collective-permute-done.5, bf16[256,4,192]{0,2,1:T(8,128)(2,1)} %collective-permute-done.4), kind=kOutput, calls=%fused_computation.24 | convolution fusion | flops 1211498496 | bytes 15335424 | tf_op jit(solution)/shard_map/tghd,sgd->tghs/dot_general | solution.py:99
  125.4 0.0 copy-done.5
  125.4 0.0 copy-start.1
  125.5 0.0 copy-start.7
  125.5 0.0 copy-start.8
  125.5 7.6 %fusion.57 = (f32[64,4,16]{0,2,1:T(8,128)S(1)}, bf16[64,4,16,768]{3,0,2,1:T(8,128)(2,1)}) fusion(f32[4,768,64,16]{1,2,3,0:T(8,128)S(1)} %fusion.18, pred[64,768]{1,0:T(8,128)(4,1)S(1)} %copy-done.5), kind=kOutput, calls=%fused_computation.87 | output fusion | flops 22020864 | bytes 18939904 | tf_op jit(solution)/shard_map/sub | solution.py:41
  133.1 0.0 collective-permute-done.2
  133.1 0.0 collective-permute-done.3
  133.1 0.0 copy-done.1
  133.1 0.0 copy-done.7
  133.1 0.0 copy-done.8
  133.1 5.2 %fusion.12 = bf16[64,4,16,128]{3,0,2,1:T(8,128)(2,1)S(1)} fusion(f32[4,128,64,16]{1,2,3,0:T(8,128)S(1)} %copy-done.1, bf16[64,4,16,768]{3,0,2,1:T(8,128)(2,1)} %get-tuple-element.16, f32[64,4,16]{0,2,1:T(8,128)S(1)} %compare_select_fusion, f32[64,4,16]{0,2,1:T(8,128)S(1)} %bitcast.122, f32[64,4,16]{0,2,1:T(8,128)S(1)} %get-tuple-element.10, ...), kind=kOutput, calls=%fused_computation.15 | convolution fusion | flops 811335680 | bytes 10305536 | tf_op jit(solution)/shard_map/tghs,sgd->tghd/dot_general | solution.py:43
  138.3 0.7 copy.68
  139.0 1.7 %copy.132 = bf16[8,8,64,128]{3,1,2,0:T(8,128)(2,1)} copy(bf16[8,8,64,128]{3,2,1,0:T(8,128)(2,1)S(1)} %bitcast.113) | data formatting | bytes 2097152
  (17 shorter events, 0.1 us)
Async XLA Ops:
  0.0 84.0 %copy-start = (bf16[4,192,192]{2,1,0:T(8,128)(2,1)S(1)}, bf16[4,192,192]{2,1,0:T(8,128)(2,1)}, u32[]{:S(2)}) copy-start(bf16[4,192,192]{2,1,0:T(8,128)(2,1)} %param.13) | copy-start | bytes 884740
  0.0 33.3 %copy-start.4 = (bf16[4,32,192]{2,1,0:T(8,128)(2,1)S(1)}, bf16[4,32,192]{2,1,0:T(8,128)(2,1)}, u32[]{:S(2)}) copy-start(bf16[4,32,192]{2,1,0:T(8,128)(2,1)} %param.12) | copy-start | bytes 147460
  8.3 25.8 %copy-start.6 = (bf16[4,32,128]{2,1,0:T(8,128)(2,1)S(1)}, bf16[4,32,128]{2,1,0:T(8,128)(2,1)}, u32[]{:S(2)}) copy-start(bf16[4,32,128]{2,1,0:T(8,128)(2,1)} %param.14) | copy-start | bytes 98308
  8.3 26.4 %copy-start.9 = (bf16[64,128]{1,0:T(8,128)(2,1)S(1)}, bf16[64,128]{1,0:T(8,128)(2,1)}, u32[]{:S(2)}) copy-start(bf16[64,128]{1,0:T(8,128)(2,1)} %param.11) | copy-start | bytes 49156
  8.4 113.5 %collective-permute-start.4 = (bf16[256,4,192]{0,2,1:T(8,128)(2,1)S(1)}, bf16[256,4,192]{0,2,1:T(8,128)(2,1)}, u32[]{:S(2)}, u32[]{:S(2)}) collective-permute-start(bf16[256,4,192]{0,2,1:T(8,128)(2,1)S(1)} %bitcast.114), channel_id=1, source_target_pairs={{0,8},{4,12},{8,16},{12,20},{16,24},{20,28},{1,9},{5,13},{9,17},{1... | collective-permute-start | bytes 1179656 | tf_op jit(solution)/shard_map/ppermute | solution.py:20
  12.7 109.3 %collective-permute-start.5 = (bf16[256,4,192]{0,2,1:T(8,128)(2,1)S(1)}, bf16[256,4,192]{0,2,1:T(8,128)(2,1)}, u32[]{:S(2)}, u32[]{:S(2)}) collective-permute-start(bf16[256,4,192]{0,2,1:T(8,128)(2,1)S(1)} %bitcast.115), channel_id=1, source_target_pairs={{0,4},{4,8},{8,12},{12,16},{16,20},{20,24},{24,28},{1,5},{5,9},{9,... | collective-permute-start | bytes 1179656 | tf_op jit(solution)/shard_map/ppermute | solution.py:20
  23.8 109.3 %collective-permute-start.2 = (bf16[256,4,128]{2,0,1:T(8,128)(2,1)}, bf16[256,4,128]{2,0,1:T(8,128)(2,1)}, u32[]{:S(2)}, u32[]{:S(2)}) collective-permute-start(bf16[256,4,128]{2,0,1:T(8,128)(2,1)} %copy.64), channel_id=1, source_target_pairs={{0,8},{4,12},{8,16},{12,20},{16,24},{20,28},{1,9},{5,13},{9,17},{1... | collective-permute-start | bytes 786440 | tf_op jit(solution)/shard_map/ppermute | solution.py:20
  26.6 106.5 %collective-permute-start.3 = (bf16[256,4,128]{2,0,1:T(8,128)(2,1)}, bf16[256,4,128]{2,0,1:T(8,128)(2,1)}, u32[]{:S(2)}, u32[]{:S(2)}) collective-permute-start(bf16[256,4,128]{2,0,1:T(8,128)(2,1)} %copy.64), channel_id=1, source_target_pairs={{0,4},{4,8},{8,12},{12,16},{16,20},{20,24},{24,28},{1,5},{5,9},{9,... | collective-permute-start | bytes 786440 | tf_op jit(solution)/shard_map/ppermute | solution.py:20
  31.4 10.9 %collective-permute-start.1 = (bf16[16,4,128]{0,2,1:T(8,128)(2,1)}, bf16[16,4,128]{0,2,1:T(8,128)(2,1)}, u32[]{:S(2)}, u32[]{:S(2)}) collective-permute-start(bf16[16,4,128]{0,2,1:T(8,128)(2,1)} %bitcast.21), channel_id=1, source_target_pairs={{4,0},{8,4},{12,8},{16,12},{20,16},{24,20},{28,24},{5,1},{9,5},{13... | collective-permute-start | bytes 49160 | tf_op jit(solution)/shard_map/ppermute | solution.py:20
  38.8 7.8 %copy-start.2 = (f32[4,128,16]{1,2,0:T(8,128)S(1)}, f32[4,128,16]{1,2,0:T(8,128)}, u32[]{:S(2)}) copy-start(f32[4,128,16]{1,2,0:T(8,128)} %get-tuple-element.12) | copy-start | bytes 98308
  38.8 7.9 %copy-start.3 = (f32[4,128,16]{1,0,2:T(4,128)S(1)}, f32[4,128,16]{1,0,2:T(4,128)}, u32[]{:S(2)}) copy-start(f32[4,128,16]{1,0,2:T(4,128)} %multiply_reduce_fusion.3) | copy-start | bytes 98308
  42.4 37.4 %collective-permute-start = (bf16[16,4,192]{0,2,1:T(8,128)(2,1)}, bf16[16,4,192]{0,2,1:T(8,128)(2,1)}, u32[]{:S(2)}, u32[]{:S(2)}) collective-permute-start(bf16[16,4,192]{0,2,1:T(8,128)(2,1)} %bitcast.11), channel_id=1, source_target_pairs={{4,0},{8,4},{12,8},{16,12},{20,16},{24,20},{28,24},{5,1},{9,5},{13... | collective-permute-start | bytes 73736 | tf_op jit(solution)/shard_map/ppermute | solution.py:20
  122.0 3.5 %copy-start.5 = (pred[64,768]{1,0:T(8,128)(4,1)S(1)}, pred[64,768]{1,0:T(8,128)(4,1)}, u32[]{:S(2)}) copy-start(pred[64,768]{1,0:T(8,128)(4,1)} %and_and_fusion) | copy-start | bytes 147460
  125.4 7.7 %copy-start.1 = (f32[4,128,64,16]{1,2,3,0:T(8,128)S(1)}, f32[4,128,64,16]{1,2,3,0:T(8,128)}, u32[]{:S(2)}) copy-start(f32[4,128,64,16]{1,2,3,0:T(8,128)} %fusion.32) | copy-start | bytes 6291460
  125.5 7.7 %copy-start.7 = (f32[64,4,16,1]{0,3,2,1:T(1,128)S(1)}, f32[64,4,16,1]{0,3,2,1:T(1,128)}, u32[]{:S(2)}) copy-start(f32[64,4,16,1]{0,3,2,1:T(1,128)} %get-tuple-element.5) | copy-start | bytes 49156
  125.5 7.7 %copy-start.8 = (f32[64,4,16,1]{0,3,2,1:T(1,128)S(1)}, f32[64,4,16,1]{0,3,2,1:T(1,128)}, u32[]{:S(2)}) copy-start(f32[64,4,16,1]{0,3,2,1:T(1,128)} %get-tuple-element.6) | copy-start | bytes 49156
where the time goes:
time: 141 us
  blocking collectives  77 us (55%)
  starting transfers between devices  17.8 us (13%)
  other arithmetic  17.8 us (13%)
  matrix products  15.4 us (11%)
  local copies, waits for them, and re-layouts  12.4 us (9%)
    all_gather x1, blocking collectives, attend(): lax.all_gather(summary_values, 'ctx', axis=0, tiled=True)  32 us
    all_gather x1, blocking collectives, attend(): lax.all_gather(summary_keys, 'ctx', axis=0, tiled=True)  30.7 us
    ppermute x6, starting transfers between devices, passed_along(): lax.ppermute(value, axis, [(source, source + steps) for source in range(l...  17.8 us
    all_gather x1, blocking collectives, local(): lax.all_gather(key_rows, 'head', axis=0, tiled=True)  8.26 us
    sub x1, other arithmetic, soft_mix(): weights = jnp.where(visible, jnp.exp(scores - highest), 0.0)  7.61 us
    all_gather x1, blocking collectives, local(): lax.all_gather(values, 'head', axis=0, tiled=True)  5.97 us
    dot_general x1, matrix products, soft_mix(): jnp.einsum('tghs,sgd->tghd', weights.astype(jnp.bfloat16), value_rows, pr...  5.2 us
    unnamed x25, local copies, waits for them, and re-layouts  4.11 us
  transfers between devices with their start and end apart: 6, of which 0 were waited for; matrix products, arithmetic and copies ran while one was open for 27% of the time, Pallas kernels for 0%

commit v1 on v0

v1 whole, which is shorter than its diff:
```python
import functools
import math

import jax
import jax.numpy as jnp
from jax import lax
from jax.experimental import pallas as pl
from jax.experimental.pallas import tpu as pltpu
from jax.sharding import Mesh, PartitionSpec as P

QHEADS = 64
GROUPS = 4
PER_GROUP = QHEADS // GROUPS
KDIM = 192
VDIM = 128
BLOCK = 32
STRIDE = 16
WINDOW = 512
KCOLS = GROUPS * KDIM
VCOLS = GROUPS * VDIM
COLS = KCOLS + VCOLS
CROWS = 8
LOG2E = 1.4426950408889634
HIDE = -1e30
HEADS_AT_ONCE = 4
WIDE = 256
AXES = ("slab", "member")


def split_hi_lo(x):
    hi = x.astype(jnp.bfloat16).astype(jnp.float32)
    return hi, x - hi


def pooled_halves(rows, mix):
    halves = rows.shape[0] // STRIDE
    cut = rows.reshape(halves, STRIDE, rows.shape[1])
    first = jnp.sum(cut * mix[None, :STRIDE], axis=1)
    second = jnp.sum(cut * mix[None, STRIDE:], axis=1)
    return first, second


def compress_rows(rows, mix_ref, proj_ref, width):
    mix = jnp.concatenate([mix_ref[g].astype(jnp.float32) for g in range(GROUPS)], axis=1)
    first, second = pooled_halves(rows.astype(jnp.float32), mix)
    count = first.shape[0]
    whole = first[: count - 1] + second[1:]
    a_hi, a_lo = split_hi_lo(first[count - 1 :])
    b_hi, b_lo = split_hi_lo(second[:1])
    pad = jnp.zeros((CROWS - (count - 1) - 4, rows.shape[1]), jnp.float32)
    stacked = jnp.concatenate([whole, a_hi, a_lo, b_hi, b_lo, pad], axis=0)
    out = []
    for g in range(GROUPS):
        part = stacked[:, g * width : (g + 1) * width].astype(jnp.bfloat16)
        out.append(jnp.dot(part, proj_ref[g], preferred_element_type=jnp.float32))
    out = jnp.concatenate(out, axis=1)
    x_hi, x_lo = split_hi_lo(out[count - 1 : count] + out[count : count + 1])
    y_hi, y_lo = split_hi_lo(out[count + 1 : count + 2] + out[count + 2 : count + 3])
    return jnp.concatenate([out[: count - 1], x_hi, x_lo, y_hi, y_lo, pad], axis=0)


def pack_kernel(k_ref, v_ref, kmix_ref, kproj_ref, vmix_ref, vproj_ref, packed_ref, small_ref):
    rows = k_ref.shape[0]
    packed_ref[:rows, :KCOLS] = k_ref[...]
    packed_ref[:rows, KCOLS:] = v_ref[...]
    ck = compress_rows(k_ref[...], kmix_ref, kproj_ref, KDIM).astype(jnp.bfloat16)
    cv = compress_rows(v_ref[...], vmix_ref, vproj_ref, VDIM).astype(jnp.bfloat16)
    small_ref[:, :KCOLS] = ck
    small_ref[:, KCOLS:] = cv
    packed_ref[rows:, :KCOLS] = ck
    packed_ref[rows:, KCOLS:] = cv


def pack(keys, values, key_mix, key_proj, value_mix, value_proj):
    rows = keys.shape[0]
    return pl.pallas_call(
        pack_kernel,
        out_shape=(
            jax.ShapeDtypeStruct((rows + CROWS, COLS), jnp.bfloat16),
            jax.ShapeDtypeStruct((CROWS, COLS), jnp.bfloat16),
        ),
        name="pack",
    )(keys, values, key_mix, key_proj, value_mix, value_proj)


def attend_kernel(slabs, members, rows, place_ref, *refs):
    pairs = members // 2 - 1
    own_ref, before_ref, mixed_ref = refs[:3]
    near_refs = refs[3 : 3 + 2 * pairs]
    far_refs = refs[3 + 2 * pairs : 3 + 2 * pairs + slabs - 1]
    q_ref, gate_ref, out_ref, ke_ref, ko_ref, vt_ref, wbias_ref, cbias_ref, crow_ref = refs[
        3 + 2 * pairs + slabs - 1 :
    ]
    slab = place_ref[0]
    member = place_ref[1]
    device = slab * members + member
    nblocks = slabs * members * (rows // STRIDE)
    per = rows // STRIDE
    wkeys = (members + 1) * rows
    half = WIDE - KDIM

    @pl.when(pl.program_id(0) == 0)
    def _():
        lane = lax.broadcasted_iota(jnp.int32, (1, WIDE), 1)

        def place_keys(at, block):
            count = block.shape[0]
            for g in range(GROUPS):
                start = g * KDIM
                lead = start % 128
                piece = block[:, start - lead : start - lead + WIDE]
                if lead == 0:
                    even = jnp.where(lane < KDIM, piece, jnp.zeros_like(piece))
                    odd = jnp.concatenate([even[:, KDIM:], even[:, :KDIM]], axis=1)
                else:
                    odd = jnp.where(lane >= half, piece, jnp.zeros_like(piece))
                    even = jnp.concatenate([odd[:, half:], odd[:, :half]], axis=1)
                ke_ref[g, at : at + count, :] = even
                ko_ref[g, at : at + count, :] = odd

        key_row = lax.broadcasted_iota(jnp.int32, (rows, 2 * rows), 0)
        token = lax.broadcasted_iota(jnp.int32, (rows, 2 * rows), 1) % rows
        sources = [(own_ref, device), (before_ref, device - members)]
        odd_member = member % 2
        sources.append((mixed_ref, jnp.where(odd_member == 1, device - 1, device - members + 1)))
        chip = member // 2
        for index in range(pairs):
            k = 2 * (index + 1)
            for swapped in range(2):
                other = jnp.bitwise_xor(member, k + swapped)
                earlier = jnp.where(other // 2 < chip, slab, slab - 1)
                sources.append((near_refs[2 * index + swapped], earlier * members + other))
        value_parts = []
        for at, (ref, base) in enumerate(sources):
            block = ref[:rows, :]
            place_keys(at * rows, block[:, :KCOLS])
            value_parts.append(block[:, KCOLS:])
            distance = (device - base) * rows + token - key_row
            seen = (distance >= 0) & (distance < WINDOW) & (base >= 0)
            wbias_ref[at * rows : (at + 1) * rows, :] = jnp.where(seen, 0.0, HIDE)
        all_values = jnp.concatenate(value_parts, axis=0)

        def put_rows(at, block):
            block = block.astype(jnp.float32)
            for c in range(COLS // 128):
                crow_ref[c, pl.ds(at, CROWS), :] = block[:, c * 128 : (c + 1) * 128]

        put_rows(slabs * members * CROWS, jnp.zeros((CROWS, COLS), jnp.float32))
        for s in range(slabs):
            at_slab = jnp.bitwise_xor(slab, s)
            at = pl.multiple_of((at_slab * members + member) * CROWS, CROWS)
            if s == 0:
                row = own_ref[rows:, :]
            else:
                row = far_refs[s - 1][...]
            put_rows(at, row)
            for ref, flip in [(mixed_ref, 1)] + [
                (near_refs[2 * index + swapped], 2 * (index + 1) + swapped)
                for index in range(pairs)
                for swapped in range(2)
            ]:
                at = (at_slab * members + jnp.bitwise_xor(member, flip)) * CROWS
                at = pl.multiple_of(at, CROWS)
                row = ref[rows + s * CROWS : rows + (s + 1) * CROWS, :]
                put_rows(at, row)
        count = slabs * members

        def kind(r, shift=0):
            rows_of = pl.ds(r + shift * CROWS, count, stride=CROWS)
            return jnp.concatenate([crow_ref[c, rows_of, :] for c in range(COLS // 128)], axis=1)

        kinds = [kind(r) for r in range(per - 1)]
        kinds.append(kind(per - 1) + kind(per) + kind(per + 1, 1) + kind(per + 2, 1))
        crows = jnp.concatenate([x.astype(jnp.bfloat16) for x in kinds], axis=0)
        place_keys(wkeys, crows[:, :KCOLS])
        all_values = jnp.concatenate([all_values, crows[:, KCOLS:]], axis=0)
        for g in range(GROUPS):
            vt_ref[g, :VDIM, :] = all_values[:, g * VDIM : (g + 1) * VDIM].T
        vt_ref[:, VDIM:, :] = jnp.ones(
            (GROUPS, vt_ref.shape[1] - VDIM, vt_ref.shape[2]), jnp.bfloat16
        )
        at = lax.broadcasted_iota(jnp.int32, (nblocks, 2 * rows), 0)
        token = device * rows + lax.broadcasted_iota(jnp.int32, (nblocks, 2 * rows), 1) % rows
        block_index = (at % count) * per + at // count
        cbias_ref[...] = jnp.where(block_index * STRIDE + BLOCK - 1 <= token, 0.0, HIDE)

    g = pl.program_id(0)
    factor = LOG2E / math.sqrt(KDIM)
    lanes = HEADS_AT_ONCE * rows

    def branch(scores, bias, value_t):
        scores = scores + jnp.concatenate([bias] * (lanes // (2 * rows)), axis=1)
        highest = jnp.maximum(jnp.max(scores, axis=0, keepdims=True), -1e29)
        weights = jnp.exp2((scores - highest) * factor).astype(jnp.bfloat16)
        mixed = jnp.dot(value_t, weights, preferred_element_type=jnp.float32)
        total = mixed[VDIM : VDIM + 1]
        return mixed[:VDIM], jnp.where(total > 0.0, total, 1.0)

    for parity in range(2):
        keys_ref = ko_ref if parity else ke_ref
        for part in range(PER_GROUP // 2 // HEADS_AT_ONCE):
            q = []
            for u in range(HEADS_AT_ONCE):
                at = (part * HEADS_AT_ONCE + u) * 2 * KDIM + parity * (2 * KDIM - WIDE)
                q.append(q_ref[:, at : at + WIDE])
            q = jnp.concatenate(q, axis=0)
            scores = lax.dot_general(
                keys_ref[g], q, (((1,), (1,)), ((), ())), preferred_element_type=jnp.float32
            )
            near, near_total = branch(scores[:wkeys], wbias_ref[...], vt_ref[g, :, :wkeys])
            far, far_total = branch(scores[wkeys:], cbias_ref[...], vt_ref[g, :, wkeys:])
            row = 2 * (parity * (PER_GROUP // 2 // HEADS_AT_ONCE) + part)
            far_gate = gate_ref[0, row : row + 1, :] / far_total
            near_gate = gate_ref[0, row + 1 : row + 2, :] / near_total
            mixed = (far * far_gate + near * near_gate).T.astype(jnp.bfloat16)
            for u in range(HEADS_AT_ONCE):
                head = 2 * (part * HEADS_AT_ONCE + u) + parity
                out_ref[:, head * VDIM : (head + 1) * VDIM] = mixed[u * rows : (u + 1) * rows]


def attend(place, own, before, mixed, near, far, queries, gates, slabs, members):
    rows = queries.shape[0]
    count = slabs * members
    nblocks = count * (rows // STRIDE)
    keys = (members + 1) * rows + nblocks
    blocks = [own, before, mixed, *near, *far]
    whole = lambda x: pl.BlockSpec(x.shape, lambda g, *_: (0,) * x.ndim)
    return pl.pallas_call(
        functools.partial(attend_kernel, slabs, members, rows),
        grid_spec=pltpu.PrefetchScalarGridSpec(
            num_scalar_prefetch=1,
            grid=(GROUPS,),
            in_specs=[whole(x) for x in blocks]
            + [
                pl.BlockSpec((rows, PER_GROUP * KDIM), lambda g, *_: (0, g)),
                pl.BlockSpec((1,) + gates.shape[1:], lambda g, *_: (g, 0, 0)),
            ],
            out_specs=pl.BlockSpec((rows, PER_GROUP * VDIM), lambda g, *_: (0, g)),
            scratch_shapes=[
                pltpu.VMEM((GROUPS, keys, WIDE), jnp.bfloat16),
                pltpu.VMEM((GROUPS, keys, WIDE), jnp.bfloat16),
                pltpu.VMEM((GROUPS, VDIM + 16, keys), jnp.bfloat16),
                pltpu.VMEM(((members + 1) * rows, 2 * rows), jnp.float32),
                pltpu.VMEM((nblocks, 2 * rows), jnp.float32),
                pltpu.VMEM((COLS // 128, (count + 1) * CROWS, 128), jnp.float32),
            ],
        ),
        out_shape=jax.ShapeDtypeStruct((rows, QHEADS * VDIM), jnp.bfloat16),
        compiler_params=pltpu.CompilerParams(vmem_limit_bytes=60 << 20),
        name="attend",
    )(place, *blocks, queries, gates)


def local(slabs, members, queries, keys, values, gate_logits, key_mix, key_proj, value_mix, value_proj):
    rows = queries.shape[0]
    devices = slabs * members
    slab = lax.axis_index("slab")
    member = lax.axis_index("member")
    send = lambda x, pairs: lax.ppermute(x, AXES, pairs)
    flip = lambda k: [(d, d ^ k) for d in range(devices)]

    def across(d):
        low = d - members
        up = d + members
        if (d // members) % 2 == 1:
            return up if up < devices else d
        return low if low >= 0 else d

    packed, small = pack(keys, values, key_mix, key_proj, value_mix, value_proj)
    from_flip = send(packed, flip(members))
    from_odd = send(packed, [(d, across(d)) for d in range(devices)])
    if slabs <= 4:
        far = [from_flip[rows:]]
        far += [send(small, flip(members * s)) for s in range(2, slabs)]
    else:
        gathered = lax.all_gather(small, "slab", axis=0)
        far = [
            lax.dynamic_index_in_dim(gathered, slab ^ s, 0, keepdims=False) for s in range(1, slabs)
        ]
    before = jnp.where(slab % 2 == 1, from_flip[:rows], from_odd[:rows])
    own = packed[:rows]
    tail = jnp.concatenate([packed[rows:], *far], axis=0)
    bits = members.bit_length() - 1
    loads = [
        jnp.concatenate([jnp.where((member >> b) % 2 == 0, own, before), tail], axis=0)
        for b in range(bits)
    ]
    mixed = send(loads[0], flip(1))
    near = []
    for k in range(2, members, 2):
        got = send(loads[k.bit_length() - 1], flip(k))
        near += [got, send(got, flip(1))]
    parts = PER_GROUP // 2 // HEADS_AT_ONCE
    gates = jax.nn.sigmoid(gate_logits.astype(jnp.float32))
    gates = gates.reshape(rows, GROUPS, parts, HEADS_AT_ONCE, 2, 2).transpose(1, 4, 2, 5, 3, 0)
    gates = gates.reshape(GROUPS, 4 * parts, HEADS_AT_ONCE * rows)
    place = jnp.stack([slab, member]).astype(jnp.int32)
    return attend(place, packed, before, mixed, near, far, queries, gates, slabs, members)


def solution(mesh):
    devices = mesh.devices.size

    def whole(queries, *rest):
        rows = queries.shape[0] // devices
        members = WINDOW // rows
        slabs = devices // members
        assert members * rows == WINDOW and slabs * members == devices
        assert members & (members - 1) == 0 and slabs & (slabs - 1) == 0
        inner = Mesh(mesh.devices.reshape(slabs, members), AXES)
        split = P(AXES, None)
        step = jax.shard_map(
            functools.partial(local, slabs, members),
            mesh=inner,
            in_specs=(split, split, split, split, P(), P(), P(), P()),
            out_specs=split,
            check_vma=False,
        )
        return step(queries, *rest)

    return whole
```

time: 141 us -> 47.2 us (0.33)
  blocking collectives: 77 us -> 0 us
  matrix products: 15.4 us -> 0 us
  Pallas kernels: 0 us -> 15.1 us
  other arithmetic: 17.8 us -> 2.71 us
  waiting for transfers between devices: 0.02 us -> 14.1 us
  local copies, waits for them, and re-layouts: 12.4 us -> 3.09 us
  starting transfers between devices: 17.8 us -> 11.7 us
    all_gather x4 -> x0, blocking collectives: 77 us -> none  [the longest x1 32 us: attend(): lax.all_gather(summary_values, 'ctx', axis=0, tiled=True)]
    dot_general x6 -> x0, matrix products: 15.4 us -> none  [the longest x1 5.2 us: soft_mix(): jnp.einsum('tghs,sgd->tghd', weights.astype(jnp.bfloat16), value_rows, pr...]
    pallas_call x0 -> x2, Pallas kernels: none -> 15.1 us  [the longest x1 12.9 us: attend(): pl.pallas_call(functools.partial(attend_kernel, slabs, members, rows), gr...]
    ppermute x6 -> x11, waiting for transfers between devices: 0.02 us -> 14.1 us  [local(): send = lambda x, pairs: lax.ppermute(x, AXES, pairs)]
    sub x3 -> x0, other arithmetic: 7.62 us -> none  [the longest x1 7.61 us: soft_mix(): weights = jnp.where(visible, jnp.exp(scores - highest), 0.0)]
    ppermute x6 -> x11, starting transfers between devices: 17.8 us -> 11.7 us  [local(): send = lambda x, pairs: lax.ppermute(x, AXES, pairs)]
    reshape x2 -> x1, local copies, waits for them, and re-layouts: 4.41 us -> 0.7 us  [local(): gates = gates.reshape(GROUPS, 4 * parts, HEADS_AT_ONCE * rows)]
    concatenate x2 -> x0, other arithmetic: 3.69 us -> none  [the longest x1 1.91 us: attend(): jnp.concatenate([block_keys, next_keys], 0)]
  transfers between devices with their start and end apart: 6 -> 11, of which waited for: 0 -> 4; matrix products, arithmetic and copies ran while one was open for 27% -> 10% of each run, Pallas kernels for 0% -> 0%
where the time goes in v1:
time: 47.2 us; the launch traced here: 46.9 us
  Pallas kernels  15.1 us (32%)
  waiting for transfers between devices  14.1 us (30%)
  starting transfers between devices  11.7 us (25%)
  local copies, waits for them, and re-layouts  3.09 us (7%)
  other arithmetic  2.71 us (6%)
    ppermute x11, waiting for transfers between devices, local(): send = lambda x, pairs: lax.ppermute(x, AXES, pairs)  14.1 us
    pallas_call x1, Pallas kernels, attend(): pl.pallas_call(functools.partial(attend_kernel, slabs, members, rows), gr...  12.9 us
    ppermute x11, starting transfers between devices, local(): send = lambda x, pairs: lax.ppermute(x, AXES, pairs)  11.7 us
    pallas_call x1, Pallas kernels, pack(): pl.pallas_call(pack_kernel, out_shape=(jax.ShapeDtypeStruct((rows + CROWS...  2.25 us
    unnamed x2, other arithmetic  2.03 us
    unnamed x24, local copies, waits for them, and re-layouts  1.66 us
  transfers between devices with their start and end apart: 11, of which 4 were waited for; matrix products, arithmetic and copies ran while one was open for 10% of the time, Pallas kernels for 0%

profile of v1, /device:TPU:0, one launch (start us, length us, event | category | flops | bytes accessed | tf_op | source)
XLA Modules:
  0.0 46.9 jit_solution(7131713281728351967)
XLA Ops:
  0.0 0.0 copy-start.10
  0.0 2.2 %pack.1 = (bf16[72,1280]{1,0:T(8,128)(2,1)}, bf16[8,1280]{1,0:T(8,128)(2,1)}) custom-call(bf16[64,768]{1,0:T(8,128)(2,1)} %k_ref.1, bf16[64,512]{1,0:T(8,128)(2,1)} %v_ref.1, bf16[4,32,192]{2,1,0:T(8,128)(2,1)} %kmix_ref.1, bf16[4,192,192]{2,1,0:T(8,128)(2,1)} %kproj_ref.1, bf16[4,32,128]{2,1,0:T(8,128)(2,1)} %vmix_ref.1, bf16[4,128,128]{2,1,0:T(8,128)(2,1)} %vproj_ref.1), custom_call_target="tpu_custom_call" | custom-call | tf_op jit(solution)/shard_map/pack/pallas_call | solution.py:76
  2.3 1.6 %collective-permute-start.1 = (bf16[72,1280]{1,0:T(8,128)(2,1)}, bf16[72,1280]{1,0:T(8,128)(2,1)S(1)}, u32[]{:S(2)}, u32[]{:S(2)}) collective-permute-start(bf16[72,1280]{1,0:T(8,128)(2,1)} %get-tuple-element.7.refs_0_), channel_id=1, source_target_pairs={{0,0},{1,1},{2,2},{3,3},{4,4},{5,5},{6,6},{7,7},{8,16},{9,17},{10,... | collective-permute-start | bytes 552968 | tf_op jit(solution)/shard_map/ppermute | solution.py:259
  3.8 5.0 %collective-permute-start = (bf16[72,1280]{1,0:T(8,128)(2,1)}, bf16[72,1280]{1,0:T(8,128)(2,1)S(1)}, u32[]{:S(2)}, u32[]{:S(2)}) collective-permute-start(bf16[72,1280]{1,0:T(8,128)(2,1)} %get-tuple-element.7.refs_0_), channel_id=1, source_target_pairs={{0,8},{1,9},{2,10},{3,11},{4,12},{5,13},{6,14},{7,15},{8,0},{9,1},... | collective-permute-start | bytes 552968 | tf_op jit(solution)/shard_map/ppermute | solution.py:259
  8.8 1.3 %collective-permute-start.3 = (bf16[8,1280]{1,0:T(8,128)(2,1)}, bf16[8,1280]{1,0:T(8,128)(2,1)S(1)}, u32[]{:S(2)}, u32[]{:S(2)}) collective-permute-start(bf16[8,1280]{1,0:T(8,128)(2,1)} %get-tuple-element.8), channel_id=1, source_target_pairs={{0,24},{1,25},{2,26},{3,27},{4,28},{5,29},{6,30},{7,31},{8,16},{9,... | collective-permute-start | bytes 61448 | tf_op jit(solution)/shard_map/ppermute | solution.py:259
  10.2 0.2 collective-permute-start.2
  10.4 0.0 collective-permute-done.1
  10.4 3.5 %collective-permute-done = bf16[72,1280]{1,0:T(8,128)(2,1)S(1)} collective-permute-done((bf16[72,1280]{1,0:T(8,128)(2,1)}, bf16[72,1280]{1,0:T(8,128)(2,1)S(1)}, u32[]{:S(2)}, u32[]{:S(2)}) %collective-permute-start) | collective-permute-done | bytes 184352 | tf_op jit(solution)/shard_map/ppermute | solution.py:259
  13.9 1.0 %select_dynamic-update-slice_fusion = (bf16[96,1280]{1,0:T(8,128)(2,1)S(1)}, bf16[64,1280]{1,0:T(8,128)(2,1)S(1)}) fusion(pred[]{:T(512)S(6)} %eq.20, bf16[72,1280]{1,0:T(8,128)(2,1)} %get-tuple-element.7.refs_0_, bf16[72,1280]{1,0:T(8,128)(2,1)S(1)} %collective-permute-done.1, bf16[72,1280]{1,0:T(8,128)(2,1)S(1)} %collective-permute-done, pred[]{:T(512)S(6)} %eq.17), kind=kLoop, calls=%fused_computation.1 | loop fusion | flops 163839 | bytes 819202
  14.9 0.0 copy-start
  14.9 1.0 %select_dynamic-update-slice_fusion.1 = (bf16[96,1280]{1,0:T(8,128)(2,1)S(1)}, bf16[96,1280]{1,0:T(8,128)(2,1)S(1)}) fusion(bf16[64,1280]{1,0:T(8,128)(2,1)S(1)} %get-tuple-element.10.refs_1_, pred[]{:T(512)S(6)} %eq.19, bf16[72,1280]{1,0:T(8,128)(2,1)} %get-tuple-element.7.refs_0_, pred[]{:T(512)S(6)} %eq.18), kind=kLoop, calls=%fused_computation.2 | loop fusion | flops 163838 | bytes 655362
  15.9 0.7 %constant_dynamic-update-slice_fusion.11 = (bf16[96,1280]{1,0:T(8,128)(2,1)S(1)}, bf16[96,1280]{1,0:T(8,128)(2,1)S(1)}, bf16[96,1280]{1,0:T(8,128)(2,1)S(1)}) fusion(bf16[96,1280]{1,0:T(8,128)(2,1)S(1)} %get-tuple-element.9, bf16[72,1280]{1,0:T(8,128)(2,1)} %get-tuple-element.7.refs_0_, bf16[96,1280]{1,0:T(8,128)(2,1)S(1)} %get-tuple-element.11, ...), kind=kLoop, calls=%fused_computation.15 | loop fusion | bytes 81920
  16.6 0.6 %fusion = (bf16[8,1280]{1,0:T(8,128)(2,1)}, bf16[96,1280]{1,0:T(8,128)(2,1)S(1)}, bf16[96,1280]{1,0:T(8,128)(2,1)S(1)}, bf16[96,1280]{1,0:T(8,128)(2,1)S(1)}) fusion(bf16[72,1280]{1,0:T(8,128)(2,1)S(1)} %collective-permute-done, bf16[96,1280]{1,0:T(8,128)(2,1)S(1)} %get-tuple-element.19, bf16[96,1280]{1,0:T(8,128)(2,1)S(1)} %get-tuple-element.18, ...), kind=kLoop, calls=%fused_computation.18 | loop fusion | bytes 102400 | tf_op jit(solution)/shard_map/slice | solution.py:273
  17.2 0.0 collective-permute-done.2.refs_10_
  17.2 0.0 copy-start.9
  17.3 0.0 collective-permute-done.3.refs_11_
  17.3 0.0 copy-start.8
  17.3 1.6 %collective-permute-start.5 = (bf16[96,1280]{1,0:T(8,128)(2,1)S(1)}, bf16[96,1280]{1,0:T(8,128)(2,1)S(1)}, u32[]{:S(2)}, u32[]{:S(2)}) collective-permute-start(bf16[96,1280]{1,0:T(8,128)(2,1)S(1)} %get-tuple-element.21), channel_id=1, source_target_pairs={{0,2},{1,3},{2,0},{3,1},{4,6},{5,7},{6,4},{7,5},{8,10},{9,11},{10,... | collective-permute-start | bytes 737288 | tf_op jit(solution)/shard_map/ppermute | solution.py:259
  18.9 1.5 %collective-permute-start.9 = (bf16[96,1280]{1,0:T(8,128)(2,1)S(1)}, bf16[96,1280]{1,0:T(8,128)(2,1)S(1)}, u32[]{:S(2)}, u32[]{:S(2)}) collective-permute-start(bf16[96,1280]{1,0:T(8,128)(2,1)S(1)} %get-tuple-element.20), channel_id=1, source_target_pairs={{0,6},{1,7},{2,4},{3,5},{4,2},{5,3},{6,0},{7,1},{8,14},{9,15},{10,... | collective-permute-start | bytes 737288 | tf_op jit(solution)/shard_map/ppermute | solution.py:259
  20.3 0.5 %collective-permute-start.7 = (bf16[96,1280]{1,0:T(8,128)(2,1)S(1)}, bf16[96,1280]{1,0:T(8,128)(2,1)S(1)}, u32[]{:S(2)}, u32[]{:S(2)}) collective-permute-start(bf16[96,1280]{1,0:T(8,128)(2,1)S(1)} %get-tuple-element.20), channel_id=1, source_target_pairs={{0,4},{1,5},{2,6},{3,7},{4,0},{5,1},{6,2},{7,3},{8,12},{9,13},{10,... | collective-permute-start | bytes 737288 | tf_op jit(solution)/shard_map/ppermute | solution.py:259
  20.9 0.0 collective-permute-start.4
  20.9 5.3 %collective-permute-done.5.refs_3_ = bf16[96,1280]{1,0:T(8,128)(2,1)S(1)} collective-permute-done((bf16[96,1280]{1,0:T(8,128)(2,1)S(1)}, bf16[96,1280]{1,0:T(8,128)(2,1)S(1)}, u32[]{:S(2)}, u32[]{:S(2)}) %collective-permute-start.5) | collective-permute-done | bytes 245792 | tf_op jit(solution)/shard_map/ppermute | solution.py:259
  26.2 0.0 copy-start.1
  26.2 0.0 collective-permute-start.6
  26.2 3.9 %collective-permute-done.9.refs_7_ = bf16[96,1280]{1,0:T(8,128)(2,1)S(1)} collective-permute-done((bf16[96,1280]{1,0:T(8,128)(2,1)S(1)}, bf16[96,1280]{1,0:T(8,128)(2,1)S(1)}, u32[]{:S(2)}, u32[]{:S(2)}) %collective-permute-start.9) | collective-permute-done | bytes 245792 | tf_op jit(solution)/shard_map/ppermute | solution.py:259
  30.1 0.0 copy-start.2
  30.1 0.0 collective-permute-start.10
  30.1 1.4 %collective-permute-done.7.refs_5_ = bf16[96,1280]{1,0:T(8,128)(2,1)S(1)} collective-permute-done((bf16[96,1280]{1,0:T(8,128)(2,1)S(1)}, bf16[96,1280]{1,0:T(8,128)(2,1)S(1)}, u32[]{:S(2)}, u32[]{:S(2)}) %collective-permute-start.7) | collective-permute-done | bytes 245792 | tf_op jit(solution)/shard_map/ppermute | solution.py:259
  31.5 0.0 copy-start.3
  31.5 0.0 collective-permute-start.8
  31.5 0.0 copy-done.10
  31.5 0.1 copy.12
  31.6 0.7 %reshape.7.refs_13_ = f32[4,8,256]{2,1,0:T(8,128)} reshape(f32[4,2,2,2,4,64]{5,4,3,2,1,0:T(4,128)S(1)} %copy.13) | data formatting | bytes 65536 | tf_op jit(solution)/shard_map/reshape | solution.py:296
  32.3 0.7 %pad_add_fusion.place_ref = s32[2]{0:T(128)} fusion(s32[1]{0:T(128)} %bitcast.1, s32[1]{0:T(128)} %bitcast), kind=kLoop, calls=%fused_computation.17 | loop fusion | flops 2 | bytes 16 | tf_op jit(solution)/shard_map/stack | solution.py:297
  33.0 0.0 collective-permute-done.4.refs_2_
  33.0 0.0 copy-start.4
  33.0 0.0 collective-permute-done.6.refs_4_
  33.0 0.0 copy-start.5
  33.0 0.0 collective-permute-done.10.refs_8_
  33.0 0.0 copy-start.6
  33.0 0.0 collective-permute-done.8.refs_6_
  33.0 0.0 copy-start.7
  33.0 0.0 copy-done
  33.1 0.0 copy-done.9
  33.1 0.0 copy-done.8
  33.1 0.0 copy-done.1
  33.1 0.0 copy-done.2
  33.1 0.0 copy-done.3
  33.1 0.6 %copy-done.4 = bf16[96,1280]{1,0:T(8,128)(2,1)} copy-done((bf16[96,1280]{1,0:T(8,128)(2,1)}, bf16[96,1280]{1,0:T(8,128)(2,1)S(1)}, u32[]{:S(2)}) %copy-start.4) | copy-done | bytes 245784
  33.7 0.1 copy-done.5
  33.8 0.1 copy-done.6
  33.9 0.1 copy-done.7
  34.0 12.9 %attend.1 = bf16[64,8192]{1,0:T(8,128)(2,1)} custom-call(s32[2]{0:T(128)} %pad_add_fusion.place_ref, bf16[72,1280]{1,0:T(8,128)(2,1)} %get-tuple-element.7.refs_0_, bf16[64,1280]{1,0:T(8,128)(2,1)} %copy-done, bf16[96,1280]{1,0:T(8,128)(2,1)} %copy-done.4, bf16[96,1280]{1,0:T(8,128)(2,1)} %copy-done.1, bf16[96,1280]{1,0:T(8,128)(2,1)} %copy-done.5, ...), custom_call_target="tpu_custom_call" | custom-call | tf_op jit(solution)/shard_map/attend/pallas_call | solution.py:228
  (4 shorter events, 0.1 us)
Async XLA Ops:
  0.0 31.5 %copy-start.10 = (bf16[64,128]{1,0:T(8,128)(2,1)S(1)}, bf16[64,128]{1,0:T(8,128)(2,1)}, u32[]{:S(2)}) copy-start(bf16[64,128]{1,0:T(8,128)(2,1)} %param.11) | copy-start | bytes 49156
  2.3 8.1 %collective-permute-start.1 = (bf16[72,1280]{1,0:T(8,128)(2,1)}, bf16[72,1280]{1,0:T(8,128)(2,1)S(1)}, u32[]{:S(2)}, u32[]{:S(2)}) collective-permute-start(bf16[72,1280]{1,0:T(8,128)(2,1)} %get-tuple-element.7.refs_0_), channel_id=1, source_target_pairs={{0,0},{1,1},{2,2},{3,3},{4,4},{5,5},{6,6},{7,7},{8,16},{9,17},{10,... | collective-permute-start | bytes 552968 | tf_op jit(solution)/shard_map/ppermute | solution.py:259
  3.8 10.0 %collective-permute-start = (bf16[72,1280]{1,0:T(8,128)(2,1)}, bf16[72,1280]{1,0:T(8,128)(2,1)S(1)}, u32[]{:S(2)}, u32[]{:S(2)}) collective-permute-start(bf16[72,1280]{1,0:T(8,128)(2,1)} %get-tuple-element.7.refs_0_), channel_id=1, source_target_pairs={{0,8},{1,9},{2,10},{3,11},{4,12},{5,13},{6,14},{7,15},{8,0},{9,1},... | collective-permute-start | bytes 552968 | tf_op jit(solution)/shard_map/ppermute | solution.py:259
  8.8 8.4 %collective-permute-start.3 = (bf16[8,1280]{1,0:T(8,128)(2,1)}, bf16[8,1280]{1,0:T(8,128)(2,1)S(1)}, u32[]{:S(2)}, u32[]{:S(2)}) collective-permute-start(bf16[8,1280]{1,0:T(8,128)(2,1)} %get-tuple-element.8), channel_id=1, source_target_pairs={{0,24},{1,25},{2,26},{3,27},{4,28},{5,29},{6,30},{7,31},{8,16},{9,... | collective-permute-start | bytes 61448 | tf_op jit(solution)/shard_map/ppermute | solution.py:259
  10.2 7.0 %collective-permute-start.2 = (bf16[8,1280]{1,0:T(8,128)(2,1)}, bf16[8,1280]{1,0:T(8,128)(2,1)S(1)}, u32[]{:S(2)}, u32[]{:S(2)}) collective-permute-start(bf16[8,1280]{1,0:T(8,128)(2,1)} %get-tuple-element.8), channel_id=1, source_target_pairs={{0,16},{1,17},{2,18},{3,19},{4,20},{5,21},{6,22},{7,23},{8,24},{9,... | collective-permute-start | bytes 61448 | tf_op jit(solution)/shard_map/ppermute | solution.py:259
  14.9 18.2 %copy-start = (bf16[64,1280]{1,0:T(8,128)(2,1)}, bf16[64,1280]{1,0:T(8,128)(2,1)S(1)}, u32[]{:S(2)}) copy-start(bf16[64,1280]{1,0:T(8,128)(2,1)S(1)} %get-tuple-element.10.refs_1_) | copy-start | bytes 491524
  17.2 15.8 %copy-start.9 = (bf16[8,1280]{1,0:T(8,128)(2,1)}, bf16[8,1280]{1,0:T(8,128)(2,1)S(1)}, u32[]{:S(2)}) copy-start(bf16[8,1280]{1,0:T(8,128)(2,1)S(1)} %collective-permute-done.2.refs_10_) | copy-start | bytes 61444
  17.3 15.8 %copy-start.8 = (bf16[8,1280]{1,0:T(8,128)(2,1)}, bf16[8,1280]{1,0:T(8,128)(2,1)S(1)}, u32[]{:S(2)}) copy-start(bf16[8,1280]{1,0:T(8,128)(2,1)S(1)} %collective-permute-done.3.refs_11_) | copy-start | bytes 61444
  17.3 8.9 %collective-permute-start.5 = (bf16[96,1280]{1,0:T(8,128)(2,1)S(1)}, bf16[96,1280]{1,0:T(8,128)(2,1)S(1)}, u32[]{:S(2)}, u32[]{:S(2)}) collective-permute-start(bf16[96,1280]{1,0:T(8,128)(2,1)S(1)} %get-tuple-element.21), channel_id=1, source_target_pairs={{0,2},{1,3},{2,0},{3,1},{4,6},{5,7},{6,4},{7,5},{8,10},{9,11},{10,... | collective-permute-start | bytes 737288 | tf_op jit(solution)/shard_map/ppermute | solution.py:259
  18.9 11.2 %collective-permute-start.9 = (bf16[96,1280]{1,0:T(8,128)(2,1)S(1)}, bf16[96,1280]{1,0:T(8,128)(2,1)S(1)}, u32[]{:S(2)}, u32[]{:S(2)}) collective-permute-start(bf16[96,1280]{1,0:T(8,128)(2,1)S(1)} %get-tuple-element.20), channel_id=1, source_target_pairs={{0,6},{1,7},{2,4},{3,5},{4,2},{5,3},{6,0},{7,1},{8,14},{9,15},{10,... | collective-permute-start | bytes 737288 | tf_op jit(solution)/shard_map/ppermute | solution.py:259
  20.3 11.1 %collective-permute-start.7 = (bf16[96,1280]{1,0:T(8,128)(2,1)S(1)}, bf16[96,1280]{1,0:T(8,128)(2,1)S(1)}, u32[]{:S(2)}, u32[]{:S(2)}) collective-permute-start(bf16[96,1280]{1,0:T(8,128)(2,1)S(1)} %get-tuple-element.20), channel_id=1, source_target_pairs={{0,4},{1,5},{2,6},{3,7},{4,0},{5,1},{6,2},{7,3},{8,12},{9,13},{10,... | collective-permute-start | bytes 737288 | tf_op jit(solution)/shard_map/ppermute | solution.py:259
  20.9 12.1 %collective-permute-start.4 = (bf16[96,1280]{1,0:T(8,128)(2,1)S(1)}, bf16[96,1280]{1,0:T(8,128)(2,1)S(1)}, u32[]{:S(2)}, u32[]{:S(2)}) collective-permute-start(bf16[96,1280]{1,0:T(8,128)(2,1)S(1)} %get-tuple-element.22), channel_id=1, source_target_pairs={{0,1},{1,0},{2,3},{3,2},{4,5},{5,4},{6,7},{7,6},{8,9},{9,8},{10,11... | collective-permute-start | bytes 737288 | tf_op jit(solution)/shard_map/ppermute | solution.py:259
  26.2 6.9 %copy-start.1 = (bf16[96,1280]{1,0:T(8,128)(2,1)}, bf16[96,1280]{1,0:T(8,128)(2,1)S(1)}, u32[]{:S(2)}) copy-start(bf16[96,1280]{1,0:T(8,128)(2,1)S(1)} %collective-permute-done.5.refs_3_) | copy-start | bytes 737284
  26.2 6.8 %collective-permute-start.6 = (bf16[96,1280]{1,0:T(8,128)(2,1)S(1)}, bf16[96,1280]{1,0:T(8,128)(2,1)S(1)}, u32[]{:S(2)}, u32[]{:S(2)}) collective-permute-start(bf16[96,1280]{1,0:T(8,128)(2,1)S(1)} %collective-permute-done.5.refs_3_), channel_id=1, source_target_pairs={{0,1},{1,0},{2,3},{3,2},{4,5},{5,4},{6,7},{7,6},{8,9},{9,8},{10,11... | collective-permute-start | bytes 737288 | tf_op jit(solution)/shard_map/ppermute | solution.py:259
  30.1 3.0 %copy-start.2 = (bf16[96,1280]{1,0:T(8,128)(2,1)}, bf16[96,1280]{1,0:T(8,128)(2,1)S(1)}, u32[]{:S(2)}) copy-start(bf16[96,1280]{1,0:T(8,128)(2,1)S(1)} %collective-permute-done.9.refs_7_) | copy-start | bytes 737284
  30.1 2.9 %collective-permute-start.10 = (bf16[96,1280]{1,0:T(8,128)(2,1)S(1)}, bf16[96,1280]{1,0:T(8,128)(2,1)S(1)}, u32[]{:S(2)}, u32[]{:S(2)}) collective-permute-start(bf16[96,1280]{1,0:T(8,128)(2,1)S(1)} %collective-permute-done.9.refs_7_), channel_id=1, source_target_pairs={{0,1},{1,0},{2,3},{3,2},{4,5},{5,4},{6,7},{7,6},{8,9},{9,8},{10,11... | collective-permute-start | bytes 737288 | tf_op jit(solution)/shard_map/ppermute | solution.py:259
  31.5 1.6 %copy-start.3 = (bf16[96,1280]{1,0:T(8,128)(2,1)}, bf16[96,1280]{1,0:T(8,128)(2,1)S(1)}, u32[]{:S(2)}) copy-start(bf16[96,1280]{1,0:T(8,128)(2,1)S(1)} %collective-permute-done.7.refs_5_) | copy-start | bytes 737284
  31.5 1.6 %collective-permute-start.8 = (bf16[96,1280]{1,0:T(8,128)(2,1)S(1)}, bf16[96,1280]{1,0:T(8,128)(2,1)S(1)}, u32[]{:S(2)}, u32[]{:S(2)}) collective-permute-start(bf16[96,1280]{1,0:T(8,128)(2,1)S(1)} %collective-permute-done.7.refs_5_), channel_id=1, source_target_pairs={{0,1},{1,0},{2,3},{3,2},{4,5},{5,4},{6,7},{7,6},{8,9},{9,8},{10,11... | collective-permute-start | bytes 737288 | tf_op jit(solution)/shard_map/ppermute | solution.py:259
  33.0 0.7 %copy-start.4 = (bf16[96,1280]{1,0:T(8,128)(2,1)}, bf16[96,1280]{1,0:T(8,128)(2,1)S(1)}, u32[]{:S(2)}) copy-start(bf16[96,1280]{1,0:T(8,128)(2,1)S(1)} %collective-permute-done.4.refs_2_) | copy-start | bytes 737284
  33.0 0.8 %copy-start.5 = (bf16[96,1280]{1,0:T(8,128)(2,1)}, bf16[96,1280]{1,0:T(8,128)(2,1)S(1)}, u32[]{:S(2)}) copy-start(bf16[96,1280]{1,0:T(8,128)(2,1)S(1)} %collective-permute-done.6.refs_4_) | copy-start | bytes 737284
  33.0 0.9 %copy-start.6 = (bf16[96,1280]{1,0:T(8,128)(2,1)}, bf16[96,1280]{1,0:T(8,128)(2,1)S(1)}, u32[]{:S(2)}) copy-start(bf16[96,1280]{1,0:T(8,128)(2,1)S(1)} %collective-permute-done.10.refs_8_) | copy-start | bytes 737284
  33.0 1.0 %copy-start.7 = (bf16[96,1280]{1,0:T(8,128)(2,1)}, bf16[96,1280]{1,0:T(8,128)(2,1)S(1)}, u32[]{:S(2)}) copy-start(bf16[96,1280]{1,0:T(8,128)(2,1)S(1)} %collective-permute-done.8.refs_6_) | copy-start | bytes 737284

commit v2 on v1

v2 whole, which is shorter than its diff:
```python
import functools
import math

import jax
import jax.numpy as jnp
from jax import lax
from jax.experimental import pallas as pl
from jax.experimental.pallas import tpu as pltpu
from jax.sharding import Mesh, PartitionSpec as P

QHEADS = 64
GROUPS = 4
PER_GROUP = QHEADS // GROUPS
KDIM = 192
VDIM = 128
BLOCK = 32
STRIDE = 16
WINDOW = 512
KCOLS = GROUPS * KDIM
VCOLS = GROUPS * VDIM
COLS = KCOLS + VCOLS
CROWS = 8
LOG2E = 1.4426950408889634
HIDE = -1e30
HEADS_AT_ONCE = 4
WIDE = 256
SUMS = 16
STATE = VDIM + SUMS
VMEM_GRANT = 40 << 20
VMEM_MOST = 63 << 20
AXES = ("slab", "member")
HALF = WIDE - KDIM
PARTS = PER_GROUP // 2 // HEADS_AT_ONCE
CHUNKS = 2 * PARTS
FACTOR = LOG2E / math.sqrt(KDIM)


def split_hi_lo(x):
    hi = x.astype(jnp.bfloat16).astype(jnp.float32)
    return hi, x - hi


def pooled_halves(rows, mix):
    halves = rows.shape[0] // STRIDE
    cut = rows.reshape(halves, STRIDE, rows.shape[1])
    first = jnp.sum(cut * mix[None, :STRIDE], axis=1)
    second = jnp.sum(cut * mix[None, STRIDE:], axis=1)
    return first, second


def compress_rows(rows, mix_ref, proj_ref, width):
    mix = jnp.concatenate([mix_ref[g].astype(jnp.float32) for g in range(GROUPS)], axis=1)
    first, second = pooled_halves(rows.astype(jnp.float32), mix)
    count = first.shape[0]
    whole = first[: count - 1] + second[1:]
    a_hi, a_lo = split_hi_lo(first[count - 1 :])
    b_hi, b_lo = split_hi_lo(second[:1])
    pad = jnp.zeros((CROWS - (count - 1) - 4, rows.shape[1]), jnp.float32)
    stacked = jnp.concatenate([whole, a_hi, a_lo, b_hi, b_lo, pad], axis=0)
    out = []
    for g in range(GROUPS):
        part = stacked[:, g * width : (g + 1) * width].astype(jnp.bfloat16)
        out.append(jnp.dot(part, proj_ref[g], preferred_element_type=jnp.float32))
    out = jnp.concatenate(out, axis=1)
    x_hi, x_lo = split_hi_lo(out[count - 1 : count] + out[count : count + 1])
    y_hi, y_lo = split_hi_lo(out[count + 1 : count + 2] + out[count + 2 : count + 3])
    return jnp.concatenate([out[: count - 1], x_hi, x_lo, y_hi, y_lo, pad], axis=0)


def pack_kernel(k_ref, v_ref, kmix_ref, kproj_ref, vmix_ref, vproj_ref, packed_ref, small_ref):
    rows = k_ref.shape[0]
    packed_ref[:rows, :KCOLS] = k_ref[...]
    packed_ref[:rows, KCOLS:] = v_ref[...]
    ck = compress_rows(k_ref[...], kmix_ref, kproj_ref, KDIM).astype(jnp.bfloat16)
    cv = compress_rows(v_ref[...], vmix_ref, vproj_ref, VDIM).astype(jnp.bfloat16)
    small_ref[:, :KCOLS] = ck
    small_ref[:, KCOLS:] = cv
    packed_ref[rows:, :KCOLS] = ck
    packed_ref[rows:, KCOLS:] = cv


def pack(keys, values, key_mix, key_proj, value_mix, value_proj):
    rows = keys.shape[0]
    return pl.pallas_call(
        pack_kernel,
        out_shape=(
            jax.ShapeDtypeStruct((rows + CROWS, COLS), jnp.bfloat16),
            jax.ShapeDtypeStruct((CROWS, COLS), jnp.bfloat16),
        ),
        name="pack",
    )(keys, values, key_mix, key_proj, value_mix, value_proj)


def load_kernel(slabs, members, own_ref, came_ref, *refs):
    rows = own_ref.shape[0] - CROWS
    far_refs = refs[: slabs - 2]
    out_refs = refs[slabs - 2 :]
    member = lax.axis_index("member")
    own = own_ref[:rows]
    before = came_ref[:rows]
    for bit, out_ref in enumerate(out_refs):
        high = (jnp.zeros((1, 1), jnp.int32) + member // 2**bit) % 2
        out_ref[:rows] = jnp.where(high == 0, own, before)
        out_ref[rows : rows + CROWS] = own_ref[rows:]
        out_ref[rows + CROWS : rows + 2 * CROWS] = came_ref[rows:]
        for index, far_ref in enumerate(far_refs):
            at = rows + (2 + index) * CROWS
            out_ref[at : at + CROWS] = far_ref[...]


def loads(own, came, far, slabs, members):
    rows = own.shape[0] - CROWS
    shape = jax.ShapeDtypeStruct((rows + slabs * CROWS, COLS), jnp.bfloat16)
    return pl.pallas_call(
        functools.partial(load_kernel, slabs, members),
        out_shape=(shape,) * (members.bit_length() - 1),
        name="loads",
    )(own, came, *far)


def fold_max(x):
    return jnp.max(x.reshape(x.shape[0] // 8, 8, x.shape[1]), axis=0)


def stage_kernel(slabs, members, rows, kinds, first, last, *refs):
    refs = list(refs)
    take = lambda count: [refs.pop(0) for _ in range(count)]
    (own_ref,) = take(1)
    source_refs = take(len(kinds))
    crow_sources = take(slabs - 1 + members - 1) if last else []
    q_ref, gate_ref = take(2)
    state_in_ref = None if first else take(1)[0]
    (out_ref,) = take(1)
    ke_ref, ko_ref, vt_ref, bias_ref, s_ref, p_ref = take(6)
    if last:
        crow_ref, cbias_ref, full_ref, sem = take(4)
    slab = lax.axis_index("slab")
    member = lax.axis_index("member")
    device = slab * members + member
    per = rows // STRIDE
    count = slabs * members
    nblocks = count * per
    wkeys = len(kinds) * rows
    keys = s_ref.shape[1]
    lanes = HEADS_AT_ONCE * rows
    lane = lax.broadcasted_iota(jnp.int32, (1, WIDE), 1)
    scalar = lambda x: jnp.zeros((1, 1), jnp.int32) + x

    def place_keys(at, block):
        size = block.shape[0]
        for g in range(GROUPS):
            start = g * KDIM
            lead = start % 128
            piece = block[:, start - lead : start - lead + WIDE]
            if lead == 0:
                even = jnp.where(lane < KDIM, piece, jnp.zeros_like(piece))
                odd = jnp.concatenate([even[:, KDIM:], even[:, :KDIM]], axis=1)
            else:
                odd = jnp.where(lane >= HALF, piece, jnp.zeros_like(piece))
                even = jnp.concatenate([odd[:, HALF:], odd[:, :HALF]], axis=1)
            ke_ref[g, at : at + size, :] = even
            ko_ref[g, at : at + size, :] = odd

    if first:
        key_row = lax.broadcasted_iota(jnp.int32, (rows, lanes), 0)
        token = lax.broadcasted_iota(jnp.int32, (rows, lanes), 1) % rows
        bias_ref[:rows, :] = jnp.where(key_row <= token, 0.0, HIDE)
        edge = (key_row > token) & (device >= members)
        bias_ref[rows:, :] = jnp.where(edge, 0.0, HIDE)
    stand_in = own_ref[:1, :]
    value_parts = []
    for at, (kind, ref) in enumerate(zip(kinds, source_refs)):
        block = ref[:rows, :]
        ones = jnp.ones((1, 1), jnp.bfloat16)
        shown, values = block[:, :KCOLS], block[:, KCOLS:]
        if kind not in ("own", "before"):
            if kind == "mixed":
                known = (scalar(member) % 2 == 1) | (scalar(slab) >= 1)
            else:
                known = (scalar(member ^ kind) // 2 < scalar(member) // 2) | (scalar(slab) >= 1)
            shown = jnp.where(known, shown, jnp.broadcast_to(stand_in[:, :KCOLS], shown.shape))
            values = jnp.where(known, values, jnp.zeros_like(values))
            ones = jnp.where(known, 1.0, 0.0).astype(jnp.bfloat16)
        place_keys(at * rows, shown)
        value_parts.append(values)
        ones = jnp.broadcast_to(ones, (SUMS, rows))
        for g in range(GROUPS):
            vt_ref[g, VDIM:, at * rows : (at + 1) * rows] = ones

    if last:

        def put_rows(at, block):
            block = block.astype(jnp.float32)
            for c in range(COLS // 128):
                crow_ref[c, pl.ds(at, CROWS), :] = block[:, c * 128 : (c + 1) * 128]

        put_rows(count * CROWS, jnp.zeros((CROWS, COLS), jnp.float32))
        for s in range(slabs):
            at_slab = jnp.where(slab >= s, slab - s, slab - s + slabs)
            if s == 0:
                row = own_ref[rows:, :]
            elif s == 1:
                row = crow_sources[0][rows:, :]
            else:
                row = crow_sources[s - 1][...]
            at = (at_slab * members + member) * CROWS
            put_rows(pl.multiple_of(at, CROWS), row)
            for flip in range(1, members):
                ref = crow_sources[slabs - 1 + flip - 1]
                at = (at_slab * members + jnp.bitwise_xor(member, flip)) * CROWS
                row = ref[rows + s * CROWS : rows + (s + 1) * CROWS, :]
                put_rows(pl.multiple_of(at, CROWS), row)

        def kind_rows(r, shift=0):
            at = pl.ds(r + shift * CROWS, count, stride=CROWS)
            return jnp.concatenate([crow_ref[c, at, :] for c in range(COLS // 128)], axis=1)

        crows = [kind_rows(r) for r in range(per - 1)]
        crows.append(
            kind_rows(per - 1) + kind_rows(per) + kind_rows(per + 1, 1) + kind_rows(per + 2, 1)
        )
        crows = jnp.concatenate([x.astype(jnp.bfloat16) for x in crows], axis=0)
        place_keys(wkeys, crows[:, :KCOLS])
        value_parts.append(crows[:, KCOLS:])
        vt_ref[:, VDIM:, wkeys:] = jnp.ones((GROUPS, SUMS, nblocks), jnp.bfloat16)
        at = lax.broadcasted_iota(jnp.int32, (nblocks, lanes), 0)
        token = device * rows + lax.broadcasted_iota(jnp.int32, (nblocks, lanes), 1) % rows
        block_index = (at % count) * per + at // count
        cbias_ref[...] = jnp.where(block_index * STRIDE + BLOCK - 1 <= token, 0.0, HIDE)

    all_values = jnp.concatenate(value_parts, axis=0)
    for g in range(GROUPS):
        vt_ref[g, :VDIM, :] = all_values[:, g * VDIM : (g + 1) * VDIM].T

    chunks = [(g, par, part) for g in range(GROUPS) for par in range(2) for part in range(PARTS)]

    def score(index, slot):
        g, parity, part = chunks[index]
        q = []
        for u in range(HEADS_AT_ONCE):
            at = g * PER_GROUP * KDIM
            at += (part * HEADS_AT_ONCE + u) * 2 * KDIM + parity * (2 * KDIM - WIDE)
            q.append(q_ref[:, at : at + WIDE])
        q = jnp.concatenate(q, axis=0)
        s = lax.dot_general(
            (ko_ref if parity else ke_ref)[g],
            q,
            (((1,), (1,)), ((), ())),
            preferred_element_type=jnp.float32,
        )
        near = s[:wkeys]
        if first:
            edge = near[: 2 * rows] + bias_ref[...]
            near = jnp.concatenate([edge, near[2 * rows :]], axis=0)
        s_ref[slot, :wkeys] = near
        near_max = jnp.max(fold_max(near), axis=0, keepdims=True)
        if not first:
            near_max = jnp.maximum(near_max, state_in_ref[index, VDIM + 1 : VDIM + 2])
        if not last:
            return (near_max,)
        far = s[wkeys:] + cbias_ref[...]
        s_ref[slot, wkeys:] = far
        return near_max, jnp.maximum(jnp.max(fold_max(far), axis=0, keepdims=True), -1e29)

    def weigh(slot, highest):
        for top, (start, stop) in zip(highest, ((0, wkeys), (wkeys, keys))):
            for at in range(start, stop, rows):
                w = jnp.exp2((s_ref[slot, at : at + rows] - top) * FACTOR)
                p_ref[slot, at : at + rows] = w.astype(jnp.bfloat16)

    def combine(index, slot, highest):
        g, parity, part = chunks[index]

        def mix(start, stop):
            return jnp.dot(
                vt_ref[g, :, start:stop],
                p_ref[slot, start:stop],
                preferred_element_type=jnp.float32,
            )

        near = mix(0, wkeys)
        if not first:
            scale = jnp.exp2((state_in_ref[index, VDIM + 1 : VDIM + 2] - highest[0]) * FACTOR)
            near_total = near[VDIM : VDIM + 1] + state_in_ref[index, VDIM : VDIM + 1] * scale
            near = near[:VDIM] + state_in_ref[index, :VDIM] * scale
        else:
            near_total = near[VDIM : VDIM + 1]
            near = near[:VDIM]
        if not last:
            out_ref[index, :VDIM] = near
            out_ref[index, VDIM : VDIM + 1] = near_total
            out_ref[index, VDIM + 1 : VDIM + 2] = highest[0]
            return
        far = mix(wkeys, keys)
        far_total = far[VDIM : VDIM + 1]
        far_total = jnp.where(far_total > 0.0, far_total, 1.0)
        row = 2 * index
        far_gate = gate_ref[row : row + 1, :] / far_total
        near_gate = gate_ref[row + 1 : row + 2, :] / near_total
        mixed = (far[:VDIM] * far_gate + near * near_gate).T.astype(jnp.bfloat16)
        for u in range(HEADS_AT_ONCE):
            head = g * PER_GROUP + 2 * (part * HEADS_AT_ONCE + u) + parity
            full_ref[:, head * VDIM : (head + 1) * VDIM] = mixed[u * rows : (u + 1) * rows]

    copies = []
    highest = score(0, 0)
    for index in range(len(chunks)):
        slot = index % 2
        if index + 1 < len(chunks):
            following = score(index + 1, 1 - slot)
        weigh(slot, highest)
        combine(index, slot, highest)
        highest = following
        if last and (index + 1) % CHUNKS == 0:
            g = index // CHUNKS
            width = PER_GROUP * VDIM
            copies.append(
                pltpu.make_async_copy(
                    full_ref.at[:, g * width : (g + 1) * width],
                    out_ref.at[:, g * width : (g + 1) * width],
                    sem.at[g],
                )
            )
            copies[-1].start()
    for copy in copies:
        copy.wait()


def stage(own, kinds, sources, crow_sources, queries, gates, state, slabs, members):
    rows = queries.shape[0]
    first = state is None
    last = crow_sources is not None
    count = slabs * members
    nblocks = count * (rows // STRIDE)
    keys = len(kinds) * rows + (nblocks if last else 0)
    lanes = HEADS_AT_ONCE * rows
    inputs = [own, *sources, *(crow_sources or []), queries, gates]
    if not first:
        inputs.append(state)
    scratch = [
        pltpu.VMEM((GROUPS, keys, WIDE), jnp.bfloat16),
        pltpu.VMEM((GROUPS, keys, WIDE), jnp.bfloat16),
        pltpu.VMEM((GROUPS, STATE, keys), jnp.bfloat16),
        pltpu.VMEM((2 * rows, lanes), jnp.float32),
        pltpu.VMEM((2, keys, lanes), jnp.float32),
        pltpu.VMEM((2, keys, lanes), jnp.bfloat16),
    ]
    if last:
        scratch += [
            pltpu.VMEM((COLS // 128, (count + 1) * CROWS, 128), jnp.float32),
            pltpu.VMEM((nblocks, lanes), jnp.float32),
            pltpu.VMEM((rows, QHEADS * VDIM), jnp.bfloat16),
            pltpu.SemaphoreType.DMA((GROUPS,)),
        ]
        out_shape = jax.ShapeDtypeStruct((rows, QHEADS * VDIM), jnp.bfloat16)
        out_spec = pl.BlockSpec(memory_space=pl.ANY)
    else:
        out_shape = jax.ShapeDtypeStruct((GROUPS * CHUNKS, VDIM + 8, lanes), jnp.float32)
        out_spec = pl.BlockSpec(memory_space=pltpu.VMEM)
    work = GROUPS * CHUNKS * lanes * keys
    return pl.pallas_call(
        functools.partial(stage_kernel, slabs, members, rows, kinds, first, last),
        out_shape=out_shape,
        in_specs=[pl.BlockSpec(memory_space=pltpu.VMEM)] * len(inputs),
        out_specs=out_spec,
        scratch_shapes=scratch,
        compiler_params=pltpu.CompilerParams(vmem_limit_bytes=VMEM_GRANT if slabs <= 4 else VMEM_MOST),
        cost_estimate=pl.CostEstimate(
            flops=2 * work * (WIDE + STATE), bytes_accessed=4 << 20, transcendentals=work
        ),
        name="stage_last" if last else "stage_first" if first else "stage_mid",
    )(*inputs)


def local(slabs, members, queries, keys, values, gate_logits, key_mix, key_proj, value_mix, value_proj):
    rows = queries.shape[0]
    devices = slabs * members
    send = lambda x, pairs: lax.ppermute(x, AXES, pairs)
    flip = lambda k: [(d, d ^ k) for d in range(devices)]
    onward = lambda k: [(d, d + k) for d in range(devices - k)]

    packed, small = pack(keys, values, key_mix, key_proj, value_mix, value_proj)
    came = send(packed, onward(members))
    if slabs <= 4:
        far = [send(small, onward(members * s)) for s in range(2, slabs)]
    else:
        slab = lax.axis_index("slab")
        gathered = lax.all_gather(small, "slab", axis=0)
        pick = lambda s: lax.dynamic_index_in_dim(gathered, (slab - s) % slabs, 0, keepdims=False)
        far = [pick(s) for s in range(2, slabs)]
    load = loads(packed, came, far, slabs, members)
    mixed = send(load[0], flip(1))
    near = {}
    for k in reversed(range(2, members, 2)):
        near[k] = send(load[k.bit_length() - 1], flip(k))
    for k in reversed(range(2, members, 2)):
        near[k + 1] = send(near[k], flip(1))
    gates = jax.nn.sigmoid(gate_logits.astype(jnp.float32))
    gates = gates.reshape(rows, GROUPS, PARTS, HEADS_AT_ONCE, 2, 2).transpose(1, 4, 2, 5, 3, 0)
    gates = gates.reshape(GROUPS * CHUNKS * 2, HEADS_AT_ONCE * rows)
    state = stage(
        packed,
        ("own", "before", "mixed"),
        [packed, came, mixed],
        None,
        queries,
        gates,
        None,
        slabs,
        members,
    )
    late = [kind for k in reversed(range(2, members, 2)) for kind in (k, k + 1)]
    crow_sources = [came, *far, mixed, *(near[k] for k in range(2, members))]
    return stage(
        packed,
        tuple(late),
        [near[k] for k in late],
        crow_sources,
        queries,
        gates,
        state,
        slabs,
        members,
    )


def solution(mesh):
    devices = mesh.devices.size

    def whole(queries, *rest):
        rows = queries.shape[0] // devices
        members = WINDOW // rows
        slabs = devices // members
        assert members * rows == WINDOW and slabs * members == devices
        assert members & (members - 1) == 0 and slabs & (slabs - 1) == 0
        inner = Mesh(mesh.devices.reshape(slabs, members), AXES)
        split = P(AXES, None)
        step = jax.shard_map(
            functools.partial(local, slabs, members),
            mesh=inner,
            in_specs=(split, split, split, split, P(), P(), P(), P()),
            out_specs=split,
            check_vma=False,
        )
        return step(queries, *rest)

    return whole
```

time: 47.2 us -> 41.9 us (0.89)
  Pallas kernels: 15.1 us -> 11.8 us
  waiting for transfers between devices: 14.1 us -> 11.4 us
  starting transfers between devices: 11.7 us -> 14.1 us
  other arithmetic: 2.71 us -> 0.73 us
    pallas_call x1 -> x3, Pallas kernels: 12.9 us -> 9.51 us  [the longest x2 7.61 us: stage(): pl.pallas_call(functools.partial(stage_kernel, slabs, members, rows, kind...]
    ppermute x11 -> x10, waiting for transfers between devices: 14.1 us -> 11.4 us  [local(): send = lambda x, pairs: lax.ppermute(x, AXES, pairs)]
    ppermute x11 -> x10, starting transfers between devices: 11.7 us -> 14.1 us  [local(): send = lambda x, pairs: lax.ppermute(x, AXES, pairs)]
    unnamed x2 -> x0, other arithmetic: 2.03 us -> none
    unnamed x24 -> x16, local copies, waits for them, and re-layouts: 1.66 us -> 3.12 us
    div x1, other arithmetic: 0.02 us -> 0.73 us  [local(): gates = jax.nn.sigmoid(gate_logits.astype(jnp.float32))]
    another operation x1 -> x0, other arithmetic: 0.66 us -> none  [local(): place = jnp.stack([slab, member]).astype(jnp.int32)]
    slice x1 -> x0, local copies, waits for them, and re-layouts: 0.61 us -> none  [local(): far = [from_flip[rows:]]]
  transfers between devices with their start and end apart: 11 -> 10, of which waited for: 4 -> 3; matrix products, arithmetic and copies ran while one was open for 10% -> 2% of each run, Pallas kernels for 0% -> 6%
where the time goes in v2:
time: 41.9 us; the launch traced here: 41.6 us
  starting transfers between devices  14.1 us (34%)
  Pallas kernels  11.8 us (28%)
  waiting for transfers between devices  11.4 us (27%)
  local copies, waits for them, and re-layouts  3.34 us (8%)
  other arithmetic  0.73 us (2%)
    ppermute x10, starting transfers between devices, local(): send = lambda x, pairs: lax.ppermute(x, AXES, pairs)  14.1 us
    ppermute x10, waiting for transfers between devices, local(): send = lambda x, pairs: lax.ppermute(x, AXES, pairs)  11.4 us
    pallas_call x2, Pallas kernels, stage(): pl.pallas_call(functools.partial(stage_kernel, slabs, members, rows, kind...  7.61 us
    unnamed x16, local copies, waits for them, and re-layouts  3.12 us
    pallas_call x1, Pallas kernels, pack(): pl.pallas_call(pack_kernel, out_shape=(jax.ShapeDtypeStruct((rows + CROWS...  2.33 us
    pallas_call x1, Pallas kernels, loads(): pl.pallas_call(functools.partial(load_kernel, slabs, members), out_shape=...  1.9 us
  transfers between devices with their start and end apart: 10, of which 3 were waited for; matrix products, arithmetic and copies ran while one was open for 2% of the time, Pallas kernels for 6%

profile of v2, /device:TPU:0, one launch (start us, length us, event | category | flops | bytes accessed | tf_op | source)
XLA Modules:
  0.0 41.6 jit_solution(17971694453181185275)
XLA Ops:
  0.0 0.0 copy-start
  0.0 2.3 %pack.1 = (bf16[72,1280]{1,0:T(8,128)(2,1)}, bf16[8,1280]{1,0:T(8,128)(2,1)}) custom-call(bf16[64,768]{1,0:T(8,128)(2,1)} %k_ref.1, bf16[64,512]{1,0:T(8,128)(2,1)} %v_ref.1, bf16[4,32,192]{2,1,0:T(8,128)(2,1)} %kmix_ref.1, bf16[4,192,192]{2,1,0:T(8,128)(2,1)} %kproj_ref.1, bf16[4,32,128]{2,1,0:T(8,128)(2,1)} %vmix_ref.1, bf16[4,128,128]{2,1,0:T(8,128)(2,1)} %vproj_ref.1), custom_call_target="tpu_custom_call" | custom-call | tf_op jit(solution)/shard_map/pack/pallas_call | solution.py:84
  2.3 5.0 %collective-permute-start = (bf16[72,1280]{1,0:T(8,128)(2,1)}, bf16[72,1280]{1,0:T(8,128)(2,1)S(1)}, u32[]{:S(2)}, u32[]{:S(2)}) collective-permute-start(bf16[72,1280]{1,0:T(8,128)(2,1)} %get-tuple-element.10.own_ref.refs_0_.refs_1_), channel_id=1, source_target_pairs={{0,8},{1,9},{2,10},{3,11},{4,12},{5,13},{6,14},{7,15},{8,16},{9,17... | collective-permute-start | bytes 552968 | tf_op jit(solution)/shard_map/ppermute | solution.py:378
  7.3 3.3 %collective-permute-start.2 = (bf16[8,1280]{1,0:T(8,128)(2,1)}, bf16[8,1280]{1,0:T(8,128)(2,1)S(1)}, u32[]{:S(2)}, u32[]{:S(2)}) collective-permute-start(bf16[8,1280]{1,0:T(8,128)(2,1)} %get-tuple-element.11), channel_id=1, source_target_pairs={{0,24},{1,25},{2,26},{3,27},{4,28},{5,29},{6,30},{7,31}} | collective-permute-start | bytes 61448 | tf_op jit(solution)/shard_map/ppermute | solution.py:378
  10.6 1.8 %collective-permute-start.1 = (bf16[8,1280]{1,0:T(8,128)(2,1)}, bf16[8,1280]{1,0:T(8,128)(2,1)S(1)}, u32[]{:S(2)}, u32[]{:S(2)}) collective-permute-start(bf16[8,1280]{1,0:T(8,128)(2,1)} %get-tuple-element.11), channel_id=1, source_target_pairs={{0,16},{1,17},{2,18},{3,19},{4,20},{5,21},{6,22},{7,23},{8,24},{9,... | collective-permute-start | bytes 61448 | tf_op jit(solution)/shard_map/ppermute | solution.py:378
  12.5 0.0 collective-permute-done.2.refs_1_.refs_9_
  12.5 0.0 copy-start.4
  12.5 1.7 %collective-permute-done.1.refs_0_.refs_8_ = bf16[8,1280]{1,0:T(8,128)(2,1)S(1)} collective-permute-done((bf16[8,1280]{1,0:T(8,128)(2,1)}, bf16[8,1280]{1,0:T(8,128)(2,1)S(1)}, u32[]{:S(2)}, u32[]{:S(2)}) %collective-permute-start.1) | collective-permute-done | bytes 20512 | tf_op jit(solution)/shard_map/ppermute | solution.py:378
  14.1 0.0 copy-start.6
  14.1 0.0 collective-permute-done.came_ref.refs_2_.refs_7_
  14.1 0.0 copy-done.4
  14.1 0.6 %copy-done.6 = bf16[8,1280]{1,0:T(8,128)(2,1)} copy-done((bf16[8,1280]{1,0:T(8,128)(2,1)}, bf16[8,1280]{1,0:T(8,128)(2,1)S(1)}, u32[]{:S(2)}) %copy-start.6) | copy-done | bytes 20504
  14.7 0.0 copy-start.2
  14.7 0.7 %copy-done.2 = bf16[72,1280]{1,0:T(8,128)(2,1)} copy-done((bf16[72,1280]{1,0:T(8,128)(2,1)}, bf16[72,1280]{1,0:T(8,128)(2,1)S(1)}, u32[]{:S(2)}) %copy-start.2) | copy-done | bytes 184344
  15.4 1.9 %loads.1 = (bf16[96,1280]{1,0:T(8,128)(2,1)}, bf16[96,1280]{1,0:T(8,128)(2,1)}, bf16[96,1280]{1,0:T(8,128)(2,1)}) custom-call(bf16[72,1280]{1,0:T(8,128)(2,1)} %get-tuple-element.10.own_ref.refs_0_.refs_1_, bf16[72,1280]{1,0:T(8,128)(2,1)} %copy-done.2, bf16[8,1280]{1,0:T(8,128)(2,1)} %copy-done.6, bf16[8,1280]{1,0:T(8,128)(2,1)} %copy-done.4), custom_call_target="tpu_custom_call" | custom-call | tf_op jit(solution)/shard_map/loads/pallas_call | solution.py:114
  17.3 1.5 %collective-permute-start.7 = (bf16[96,1280]{1,0:T(8,128)(2,1)}, bf16[96,1280]{1,0:T(8,128)(2,1)S(1)}, u32[]{:S(2)}, u32[]{:S(2)}) collective-permute-start(bf16[96,1280]{1,0:T(8,128)(2,1)} %get-tuple-element.13), channel_id=1, source_target_pairs={{0,2},{1,3},{2,0},{3,1},{4,6},{5,7},{6,4},{7,5},{8,10},{9,11},{10,... | collective-permute-start | bytes 737288 | tf_op jit(solution)/shard_map/ppermute | solution.py:378
  18.8 1.5 %collective-permute-start.5 = (bf16[96,1280]{1,0:T(8,128)(2,1)}, bf16[96,1280]{1,0:T(8,128)(2,1)S(1)}, u32[]{:S(2)}, u32[]{:S(2)}) collective-permute-start(bf16[96,1280]{1,0:T(8,128)(2,1)} %get-tuple-element.12), channel_id=1, source_target_pairs={{0,4},{1,5},{2,6},{3,7},{4,0},{5,1},{6,2},{7,3},{8,12},{9,13},{10,... | collective-permute-start | bytes 737288 | tf_op jit(solution)/shard_map/ppermute | solution.py:378
  20.3 0.5 %collective-permute-start.3 = (bf16[96,1280]{1,0:T(8,128)(2,1)}, bf16[96,1280]{1,0:T(8,128)(2,1)S(1)}, u32[]{:S(2)}, u32[]{:S(2)}) collective-permute-start(bf16[96,1280]{1,0:T(8,128)(2,1)} %get-tuple-element.12), channel_id=1, source_target_pairs={{0,6},{1,7},{2,4},{3,5},{4,2},{5,3},{6,0},{7,1},{8,14},{9,15},{10,... | collective-permute-start | bytes 737288 | tf_op jit(solution)/shard_map/ppermute | solution.py:378
  20.8 0.0 collective-permute-start.9
  20.8 5.5 %collective-permute-done.7.refs_5_.refs_11_ = bf16[96,1280]{1,0:T(8,128)(2,1)S(1)} collective-permute-done((bf16[96,1280]{1,0:T(8,128)(2,1)}, bf16[96,1280]{1,0:T(8,128)(2,1)S(1)}, u32[]{:S(2)}, u32[]{:S(2)}) %collective-permute-start.7) | collective-permute-done | bytes 245792 | tf_op jit(solution)/shard_map/ppermute | solution.py:378
  26.3 0.0 collective-permute-start.8
  26.3 4.2 %collective-permute-done.5.refs_3_.refs_13_ = bf16[96,1280]{1,0:T(8,128)(2,1)S(1)} collective-permute-done((bf16[96,1280]{1,0:T(8,128)(2,1)}, bf16[96,1280]{1,0:T(8,128)(2,1)S(1)}, u32[]{:S(2)}, u32[]{:S(2)}) %collective-permute-start.5) | collective-permute-done | bytes 245792 | tf_op jit(solution)/shard_map/ppermute | solution.py:378
  30.6 0.0 collective-permute-start.6
  30.6 0.0 collective-permute-done.3.refs_1_.refs_15_
  30.6 0.5 %collective-permute-start.4 = (bf16[96,1280]{1,0:T(8,128)(2,1)S(1)}, bf16[96,1280]{1,0:T(8,128)(2,1)S(1)}, u32[]{:S(2)}, u32[]{:S(2)}) collective-permute-start(bf16[96,1280]{1,0:T(8,128)(2,1)S(1)} %collective-permute-done.3.refs_1_.refs_15_), channel_id=1, source_target_pairs={{0,1},{1,0},{2,3},{3,2},{4,5},{5,4},{6,7},{7,6},{8,9},{9,8},{10,11... | collective-permute-start | bytes 737288 | tf_op jit(solution)/shard_map/ppermute | solution.py:378
  31.1 0.7 %add_divide_fusion = f32[64,128]{1,0:T(8,128)S(1)} fusion(bf16[64,128]{1,0:T(8,128)(2,1)} %param.11), kind=kLoop, calls=%fused_computation | loop fusion | flops 32768 | bytes 49152 | tf_op jit(solution)/shard_map/div | solution.py:398
  31.8 0.1 copy.12
  31.9 0.1 reshape.7.refs_5_.refs_18_
  32.0 0.0 collective-permute-done.9.refs_3_.refs_10_
  32.0 0.0 copy-done
  32.0 0.0 copy-start.1
  32.0 0.9 %copy-done.1 = bf16[72,1280]{1,0:T(8,128)(2,1)S(1)} copy-done((bf16[72,1280]{1,0:T(8,128)(2,1)S(1)}, bf16[72,1280]{1,0:T(8,128)(2,1)}, u32[]{:S(2)}) %copy-start.1) | copy-done | bytes 184344
  33.0 0.0 copy-start.3
  33.0 0.9 %copy-done.3 = bf16[72,1280]{1,0:T(8,128)(2,1)S(1)} copy-done((bf16[72,1280]{1,0:T(8,128)(2,1)S(1)}, bf16[72,1280]{1,0:T(8,128)(2,1)}, u32[]{:S(2)}) %copy-start.3) | copy-done | bytes 184344
  33.9 0.0 copy-start.5
  33.9 0.0 copy-start.7
  33.9 2.3 %stage_first.1.refs_19_ = f32[16,136,256]{2,1,0:T(8,128)S(1)} custom-call(bf16[72,1280]{1,0:T(8,128)(2,1)S(1)} %copy-done.1, bf16[72,1280]{1,0:T(8,128)(2,1)S(1)} %copy-done.1, bf16[72,1280]{1,0:T(8,128)(2,1)S(1)} %copy-done.3, bf16[96,1280]{1,0:T(8,128)(2,1)S(1)} %collective-permute-done.9.refs_3_.refs_10_, bf16[64,12288]{1,0:T(8,128)(2,1)S(1)} %copy-done, ...), custom_call_target="tpu_custom_call" | custom-call | flops 629145600 | bytes 4194304 | tf_op jit(solution)/shard_map/stage_first/pallas_call | solution.py:361
  36.2 0.0 collective-permute-done.8.refs_6_.refs_12_
  36.2 0.0 collective-permute-done.6.refs_4_.refs_14_
  36.2 0.0 collective-permute-done.4.refs_2_.refs_16_
  36.2 0.0 copy-done.5
  36.2 0.0 copy-done.7
  36.3 5.3 %stage_last.1 = bf16[64,8192]{1,0:T(8,128)(2,1)} custom-call(bf16[72,1280]{1,0:T(8,128)(2,1)S(1)} %copy-done.1, bf16[96,1280]{1,0:T(8,128)(2,1)S(1)} %collective-permute-done.3.refs_1_.refs_15_, bf16[96,1280]{1,0:T(8,128)(2,1)S(1)} %collective-permute-done.4.refs_2_.refs_16_, bf16[96,1280]{1,0:T(8,128)(2,1)S(1)} %collective-permute-done.5.refs_3_.refs_13_, ...), custom_call_target="tpu_custom_call" | custom-call | flops 1677721600 | bytes 4194304 | tf_op jit(solution)/shard_map/stage_last/pallas_call | solution.py:361
  (1 shorter events, 0.0 us)
Async XLA Ops:
  0.0 32.0 %copy-start = (bf16[64,12288]{1,0:T(8,128)(2,1)S(1)}, bf16[64,12288]{1,0:T(8,128)(2,1)}, u32[]{:S(2)}) copy-start(bf16[64,12288]{1,0:T(8,128)(2,1)} %refs_17_.1) | copy-start | bytes 4718596
  2.3 11.8 %collective-permute-start = (bf16[72,1280]{1,0:T(8,128)(2,1)}, bf16[72,1280]{1,0:T(8,128)(2,1)S(1)}, u32[]{:S(2)}, u32[]{:S(2)}) collective-permute-start(bf16[72,1280]{1,0:T(8,128)(2,1)} %get-tuple-element.10.own_ref.refs_0_.refs_1_), channel_id=1, source_target_pairs={{0,8},{1,9},{2,10},{3,11},{4,12},{5,13},{6,14},{7,15},{8,16},{9,17... | collective-permute-start | bytes 552968 | tf_op jit(solution)/shard_map/ppermute | solution.py:378
  7.3 5.2 %collective-permute-start.2 = (bf16[8,1280]{1,0:T(8,128)(2,1)}, bf16[8,1280]{1,0:T(8,128)(2,1)S(1)}, u32[]{:S(2)}, u32[]{:S(2)}) collective-permute-start(bf16[8,1280]{1,0:T(8,128)(2,1)} %get-tuple-element.11), channel_id=1, source_target_pairs={{0,24},{1,25},{2,26},{3,27},{4,28},{5,29},{6,30},{7,31}} | collective-permute-start | bytes 61448 | tf_op jit(solution)/shard_map/ppermute | solution.py:378
  10.6 3.5 %collective-permute-start.1 = (bf16[8,1280]{1,0:T(8,128)(2,1)}, bf16[8,1280]{1,0:T(8,128)(2,1)S(1)}, u32[]{:S(2)}, u32[]{:S(2)}) collective-permute-start(bf16[8,1280]{1,0:T(8,128)(2,1)} %get-tuple-element.11), channel_id=1, source_target_pairs={{0,16},{1,17},{2,18},{3,19},{4,20},{5,21},{6,22},{7,23},{8,24},{9,... | collective-permute-start | bytes 61448 | tf_op jit(solution)/shard_map/ppermute | solution.py:378
  12.5 1.7 %copy-start.4 = (bf16[8,1280]{1,0:T(8,128)(2,1)}, bf16[8,1280]{1,0:T(8,128)(2,1)S(1)}, u32[]{:S(2)}) copy-start(bf16[8,1280]{1,0:T(8,128)(2,1)S(1)} %collective-permute-done.2.refs_1_.refs_9_) | copy-start | bytes 61444
  14.1 0.6 %copy-start.6 = (bf16[8,1280]{1,0:T(8,128)(2,1)}, bf16[8,1280]{1,0:T(8,128)(2,1)S(1)}, u32[]{:S(2)}) copy-start(bf16[8,1280]{1,0:T(8,128)(2,1)S(1)} %collective-permute-done.1.refs_0_.refs_8_) | copy-start | bytes 61444
  14.7 0.7 %copy-start.2 = (bf16[72,1280]{1,0:T(8,128)(2,1)}, bf16[72,1280]{1,0:T(8,128)(2,1)S(1)}, u32[]{:S(2)}) copy-start(bf16[72,1280]{1,0:T(8,128)(2,1)S(1)} %collective-permute-done.came_ref.refs_2_.refs_7_) | copy-start | bytes 552964
  17.3 9.0 %collective-permute-start.7 = (bf16[96,1280]{1,0:T(8,128)(2,1)}, bf16[96,1280]{1,0:T(8,128)(2,1)S(1)}, u32[]{:S(2)}, u32[]{:S(2)}) collective-permute-start(bf16[96,1280]{1,0:T(8,128)(2,1)} %get-tuple-element.13), channel_id=1, source_target_pairs={{0,2},{1,3},{2,0},{3,1},{4,6},{5,7},{6,4},{7,5},{8,10},{9,11},{10,... | collective-permute-start | bytes 737288 | tf_op jit(solution)/shard_map/ppermute | solution.py:378
  18.8 11.8 %collective-permute-start.5 = (bf16[96,1280]{1,0:T(8,128)(2,1)}, bf16[96,1280]{1,0:T(8,128)(2,1)S(1)}, u32[]{:S(2)}, u32[]{:S(2)}) collective-permute-start(bf16[96,1280]{1,0:T(8,128)(2,1)} %get-tuple-element.12), channel_id=1, source_target_pairs={{0,4},{1,5},{2,6},{3,7},{4,0},{5,1},{6,2},{7,3},{8,12},{9,13},{10,... | collective-permute-start | bytes 737288 | tf_op jit(solution)/shard_map/ppermute | solution.py:378
  20.3 10.2 %collective-permute-start.3 = (bf16[96,1280]{1,0:T(8,128)(2,1)}, bf16[96,1280]{1,0:T(8,128)(2,1)S(1)}, u32[]{:S(2)}, u32[]{:S(2)}) collective-permute-start(bf16[96,1280]{1,0:T(8,128)(2,1)} %get-tuple-element.12), channel_id=1, source_target_pairs={{0,6},{1,7},{2,4},{3,5},{4,2},{5,3},{6,0},{7,1},{8,14},{9,15},{10,... | collective-permute-start | bytes 737288 | tf_op jit(solution)/shard_map/ppermute | solution.py:378
  20.8 11.2 %collective-permute-start.9 = (bf16[96,1280]{1,0:T(8,128)(2,1)}, bf16[96,1280]{1,0:T(8,128)(2,1)S(1)}, u32[]{:S(2)}, u32[]{:S(2)}) collective-permute-start(bf16[96,1280]{1,0:T(8,128)(2,1)} %get-tuple-element.14), channel_id=1, source_target_pairs={{0,1},{1,0},{2,3},{3,2},{4,5},{5,4},{6,7},{7,6},{8,9},{9,8},{10,11... | collective-permute-start | bytes 737288 | tf_op jit(solution)/shard_map/ppermute | solution.py:378
  26.3 9.9 %collective-permute-start.8 = (bf16[96,1280]{1,0:T(8,128)(2,1)S(1)}, bf16[96,1280]{1,0:T(8,128)(2,1)S(1)}, u32[]{:S(2)}, u32[]{:S(2)}) collective-permute-start(bf16[96,1280]{1,0:T(8,128)(2,1)S(1)} %collective-permute-done.7.refs_5_.refs_11_), channel_id=1, source_target_pairs={{0,1},{1,0},{2,3},{3,2},{4,5},{5,4},{6,7},{7,6},{8,9},{9,8},{10,11... | collective-permute-start | bytes 737288 | tf_op jit(solution)/shard_map/ppermute | solution.py:378
  30.6 5.7 %collective-permute-start.6 = (bf16[96,1280]{1,0:T(8,128)(2,1)S(1)}, bf16[96,1280]{1,0:T(8,128)(2,1)S(1)}, u32[]{:S(2)}, u32[]{:S(2)}) collective-permute-start(bf16[96,1280]{1,0:T(8,128)(2,1)S(1)} %collective-permute-done.5.refs_3_.refs_13_), channel_id=1, source_target_pairs={{0,1},{1,0},{2,3},{3,2},{4,5},{5,4},{6,7},{7,6},{8,9},{9,8},{10,11... | collective-permute-start | bytes 737288 | tf_op jit(solution)/shard_map/ppermute | solution.py:378
  30.6 5.7 %collective-permute-start.4 = (bf16[96,1280]{1,0:T(8,128)(2,1)S(1)}, bf16[96,1280]{1,0:T(8,128)(2,1)S(1)}, u32[]{:S(2)}, u32[]{:S(2)}) collective-permute-start(bf16[96,1280]{1,0:T(8,128)(2,1)S(1)} %collective-permute-done.3.refs_1_.refs_15_), channel_id=1, source_target_pairs={{0,1},{1,0},{2,3},{3,2},{4,5},{5,4},{6,7},{7,6},{8,9},{9,8},{10,11... | collective-permute-start | bytes 737288 | tf_op jit(solution)/shard_map/ppermute | solution.py:378
  32.0 0.9 %copy-start.1 = (bf16[72,1280]{1,0:T(8,128)(2,1)S(1)}, bf16[72,1280]{1,0:T(8,128)(2,1)}, u32[]{:S(2)}) copy-start(bf16[72,1280]{1,0:T(8,128)(2,1)} %get-tuple-element.10.own_ref.refs_0_.refs_1_) | copy-start | bytes 552964
  33.0 0.9 %copy-start.3 = (bf16[72,1280]{1,0:T(8,128)(2,1)S(1)}, bf16[72,1280]{1,0:T(8,128)(2,1)}, u32[]{:S(2)}) copy-start(bf16[72,1280]{1,0:T(8,128)(2,1)} %copy-done.2) | copy-start | bytes 552964
  33.9 2.3 %copy-start.5 = (bf16[8,1280]{1,0:T(8,128)(2,1)S(1)}, bf16[8,1280]{1,0:T(8,128)(2,1)}, u32[]{:S(2)}) copy-start(bf16[8,1280]{1,0:T(8,128)(2,1)} %copy-done.4) | copy-start | bytes 61444
  33.9 2.4 %copy-start.7 = (bf16[8,1280]{1,0:T(8,128)(2,1)S(1)}, bf16[8,1280]{1,0:T(8,128)(2,1)}, u32[]{:S(2)}) copy-start(bf16[8,1280]{1,0:T(8,128)(2,1)} %copy-done.6) | copy-start | bytes 61444
